TPU v7x, 512 devices: a whole 4x4x16 slice. The times are simulated.
512 devices in a mesh: gx: 64 (over z, y), gz: 8 (over x, core).
Axes of the slice: x: 4, y: 4, z: 16, core: 2. Of those that a mesh axis runs over, the one named last changes fastest.
Arguments:
- tokens: bfloat16 [4, 256, 64, 768], P(None, 'gx', 'gz'), may hold values from -60 to 60
- cross_qkv: bfloat16 [768, 2304], P(None, 'gx'), may hold values from -16 to 16
- cross_out: bfloat16 [768, 768], P('gx'), may hold values from -0.21875 to 0.21875
- depth_qkv: bfloat16 [768, 2304], P(None, 'gx'), may hold values from -16 to 16
- depth_out: bfloat16 [768, 768], P('gx'), may hold values from -0.21875 to 0.21875
- up_proj: bfloat16 [768, 3072], P(None, 'gz'), may hold values from -0.21875 to 0.21875
- down_proj: bfloat16 [3072, 768], P('gz'), may hold values from -0.109375 to 0.109375
- gains: float32 [3, 768], replicated, may hold values from 0.5 to 1.5
- head_weight: float32 [768], replicated, may hold values from -0.21875 to 0.21875
- head_bias: float32 [1], replicated, may hold values from -1 to 1
Outputs:
- features: bfloat16 [4, 256, 64, 768], P(None, 'gx', 'gz')
- geotime: float32 [4, 256, 64], P(None, 'gx', 'gz')
All inputs are finite; a program needn't handle non-finite values.
Results may differ from a plain program's by a relative error of at most 0.013.
Values may be sent and summed in bfloat16 or wider, within the bound.
A program may use at most 64 MiB of HBM per device.

v0:
```python
import math

import jax
import jax.numpy as jnp
from jax import lax
from jax.sharding import PartitionSpec as P

HDIM = 64


log_span = math.log(256.0)


def carried_in(shard, axis, combine, identity):
    peers, position = (lax.axis_size(axis), lax.axis_index(axis))
    everything = lax.all_gather(shard, axis)
    start = jnp.broadcast_to(jnp.asarray(identity, shard.dtype), shard.shape)

    def step(k, before):
        reached = k < position
        new = combine(before, everything[k])
        return jnp.where(reached, new, before)

    return lax.fori_loop(0, peers, step, start)


def encodings(inlines, crosslines, depths, cross_start, depth_start, model_width):
    pairs = model_width // 2
    index = jnp.arange(pairs)
    freq = math.pi * jnp.exp(-log_span * index.astype(jnp.float32) / pairs)
    which = index % 3
    inline_pos = jnp.arange(inlines).astype(jnp.float32)[:, None, None, None]
    cross_pos = (cross_start + jnp.arange(crosslines)).astype(jnp.float32)[None, :, None, None]
    depth_pos = (depth_start + jnp.arange(depths)).astype(jnp.float32)[None, None, :, None]
    zeros = jnp.zeros((inlines, crosslines, depths, pairs), jnp.float32)
    position = jnp.where(
        which == 0, inline_pos + zeros, jnp.where(which == 1, cross_pos + zeros, depth_pos + zeros)
    )
    angle = position * freq
    return jnp.stack([jnp.sin(angle), jnp.cos(angle)], -1).reshape(
        inlines, crosslines, depths, model_width
    )


def normalize(stream, gain):
    scale = lax.rsqrt(jnp.mean(stream * stream, -1, keepdims=True) + 1e-05)
    return (stream * scale * gain).astype(jnp.bfloat16)


def attend(queries, keys, values):
    scale = queries.shape[-1] ** (-0.5)
    scores = (
        jnp.einsum("...qe,...ke->...qk", queries, keys, preferred_element_type=jnp.float32) * scale
    )
    scores = scores - jnp.max(scores, -1, keepdims=True)
    expo = jnp.exp(scores)
    weights = (expo / jnp.sum(expo, -1, keepdims=True)).astype(jnp.bfloat16)
    mixed = jnp.einsum("...qk,...ke->...qe", weights, values, preferred_element_type=jnp.float32)
    return mixed.astype(jnp.bfloat16)


def attend_items(trio):
    return attend(trio[0], trio[1], trio[2])


def body(
    tokens,
    cross_qkv,
    cross_out,
    depth_qkv,
    depth_out,
    up_proj,
    down_proj,
    gains,
    head_weight,
    head_bias,
):
    inlines, cross_dev, depth_dev, model_width = tokens.shape
    tok_rows = inlines * cross_dev * depth_dev
    head_count = model_width // HDIM
    cross_group = lax.axis_size("gx")
    encoding = encodings(
        inlines,
        cross_dev,
        depth_dev,
        lax.axis_index("gx") * cross_dev,
        lax.axis_index("gz") * depth_dev,
        model_width,
    )
    stream = (tokens.astype(jnp.float32) + encoding).reshape(tok_rows, model_width)
    normed = normalize(stream, gains[0])
    packed = jnp.dot(
        normed,
        lax.all_gather(cross_qkv, "gx", axis=1, tiled=True),
        preferred_element_type=jnp.float32,
    ).astype(jnp.bfloat16)
    packed = packed.reshape(inlines, cross_dev, depth_dev, 3, head_count, HDIM)
    lined = jnp.transpose(packed, (3, 0, 2, 4, 1, 5))
    per_item = inlines * depth_dev * head_count // cross_group
    lined = lined.reshape(3, cross_group, per_item, cross_dev, HDIM)
    mixed = attend_items(
        (
            lax.all_to_all(lined[0], "gx", split_axis=0, concat_axis=2, tiled=True),
            lax.all_to_all(lined[1], "gx", split_axis=0, concat_axis=2, tiled=True),
            lax.all_to_all(lined[2], "gx", split_axis=0, concat_axis=2, tiled=True),
        )
    )
    mixed = lax.all_to_all(mixed, "gx", split_axis=2, concat_axis=0, tiled=True)
    mixed = jnp.transpose(
        mixed.reshape(inlines, depth_dev, head_count, cross_dev, HDIM), (0, 3, 1, 2, 4)
    ).reshape(tok_rows, model_width)
    columns = mixed
    stream = stream + jnp.dot(
        columns,
        lax.all_gather(cross_out, "gx", axis=0, tiled=True),
        preferred_element_type=jnp.float32,
    )
    normed = normalize(stream, gains[1])
    packed = jnp.dot(
        normed,
        lax.all_gather(depth_qkv, "gx", axis=1, tiled=True),
        preferred_element_type=jnp.float32,
    ).astype(jnp.bfloat16)
    packed = packed.reshape(inlines, cross_dev, depth_dev, 3, head_count, HDIM)
    lined = jnp.transpose(packed, (3, 0, 1, 4, 2, 5))
    all_keys, all_values = (
        lax.all_gather(lined[1], "gz", axis=3, tiled=True),
        lax.all_gather(lined[2], "gz", axis=3, tiled=True),
    )
    mixed = attend(lined[0], all_keys, all_values)
    mixed = jnp.transpose(mixed, (0, 1, 3, 2, 4)).reshape(tok_rows, model_width)
    columns = mixed
    stream = stream + jnp.dot(
        columns,
        lax.all_gather(depth_out, "gx", axis=0, tiled=True),
        preferred_element_type=jnp.float32,
    )
    normed = normalize(stream, gains[2])
    hidden = jax.nn.gelu(
        jnp.dot(
            lax.all_gather(normed, "gz", axis=0, tiled=True),
            up_proj,
            preferred_element_type=jnp.float32,
        )
    ).astype(jnp.bfloat16)
    stream = stream + lax.psum_scatter(
        jnp.dot(hidden, down_proj, preferred_element_type=jnp.float32).astype(jnp.bfloat16),
        "gz",
        scatter_dimension=0,
        tiled=True,
    ).astype(jnp.float32)
    features = stream.astype(jnp.bfloat16).reshape(inlines, cross_dev, depth_dev, model_width)
    thickness = jax.nn.softplus(
        jnp.dot(stream, head_weight, precision=lax.Precision.HIGHEST) + head_bias[0]
    )
    local_time = jnp.cumsum(thickness.reshape(inlines, cross_dev, depth_dev), axis=2)
    line_total = local_time[:, :, -1]
    carried = carried_in(
        line_total, "gz", lambda earlier, later: earlier + later, jnp.zeros_like(line_total)
    )
    geotime = local_time + carried[:, :, None]
    return (features, geotime)


def solution(mesh):
    return jax.shard_map(
        body,
        mesh=mesh,
        in_specs=(
            P(None, "gx", "gz", None),
            P(None, "gx"),
            P("gx", None),
            P(None, "gx"),
            P("gx", None),
            P(None, "gz"),
            P("gz", None),
            P(),
            P(),
            P(),
        ),
        out_specs=(P(None, "gx", "gz", None), P(None, "gx", "gz")),
        check_vma=False,
    )
```

profile of v0, /device:TPU:1, one launch (start us, length us, event | category | flops | bytes accessed | tf_op | source)
XLA Modules:
  0.0 772.2 jit_solution(6534772506447443359)
XLA Ops:
  10.3 6.4 copy.57
  16.6 4.4 copy.58
  21.4 132.3 %all-gather.21.cloned.1.call-done = bf16[64,36,768]{2,1,0:T(8,128)(2,1)} async-done(((bf16[1,36,768]{2,1,0:T(8,128)(2,1)}), bf16[64,36,768]{2,1,0:T(8,128)(2,1)}) %all-gather.21.cloned.1.call-update) | async-done | bytes 3538960 | tf_op jit(solution)/shard_map/all_gather | solution.py:94
  153.7 6.2 reshape.159
  159.8 3.3 convolution_convert_fusion.1
  164.1 1.1 fusion.53
  166.5 8.7 %all-to-all-start.1 = ((bf16[64,2,768]{2,1,0:T(2,128)(2,1)}), bf16[64,2,768]{2,1,0:T(2,128)(2,1)S(1)}, u32[]{:S(2)}, u32[]{:S(2)}) async-start(bf16[64,2,768]{2,1,0:T(2,128)(2,1)} %reshape.175), calls=%async_computation.1 | async-start | bytes 393216 | tf_op jit(solution)/shard_map/all_to_all | solution.py:104
  176.5 15.4 %all-to-all-done.1 = bf16[64,2,768]{2,1,0:T(2,128)(2,1)S(1)} async-done(((bf16[64,2,768]{2,1,0:T(2,128)(2,1)}), bf16[64,2,768]{2,1,0:T(2,128)(2,1)S(1)}, u32[]{:S(2)}, u32[]{:S(2)}) %all-to-all-start.1) | async-done | bytes 196640 | tf_op jit(solution)/shard_map/all_to_all | solution.py:104
  191.9 4.6 all-to-all-start
  197.7 15.1 %all-to-all-done = bf16[64,2,768]{2,1,0:T(2,128)(2,1)S(1)} async-done(((bf16[64,2,768]{2,1,0:T(2,128)(2,1)}), bf16[64,2,768]{2,1,0:T(2,128)(2,1)S(1)}, u32[]{:S(2)}, u32[]{:S(2)}) %all-to-all-start) | async-done | bytes 196640 | tf_op jit(solution)/shard_map/all_to_all | solution.py:103
  212.9 4.6 all-to-all-start.2
  218.9 15.0 %all-to-all-done.2 = bf16[64,2,768]{2,1,0:T(2,128)(2,1)S(1)} async-done(((bf16[64,2,768]{2,1,0:T(2,128)(2,1)}), bf16[64,2,768]{2,1,0:T(2,128)(2,1)S(1)}, u32[]{:S(2)}, u32[]{:S(2)}) %all-to-all-start.2) | async-done | bytes 196640 | tf_op jit(solution)/shard_map/all_to_all | solution.py:105
  234.4 1.8 fusion.55
  236.2 1.7 fusion.27
  239.2 4.6 all-to-all-start.3
  244.1 49.5 %all-gather.23.cloned.1.call-done = bf16[64,12,768]{2,1,0:T(8,128)(2,1)} async-done(((bf16[1,12,768]{2,1,0:T(8,128)(2,1)}), bf16[64,12,768]{2,1,0:T(8,128)(2,1)}) %all-gather.23.cloned.1.call-update) | async-done | bytes 1179664 | tf_op jit(solution)/shard_map/all_gather | solution.py:115
  293.6 2.2 reshape.161
  295.9 142.8 %all-gather.25.cloned.1.call-done = bf16[64,36,768]{2,1,0:T(8,128)(2,1)} async-done(((bf16[1,36,768]{2,1,0:T(8,128)(2,1)}), bf16[64,36,768]{2,1,0:T(8,128)(2,1)}) %all-gather.25.cloned.1.call-update) | async-done | bytes 3538960 | tf_op jit(solution)/shard_map/all_gather | solution.py:121
  438.7 6.2 reshape.163
  447.0 3.3 convolution_convert_fusion
  453.2 122.6 %all-gather.27.cloned.1.call-done = bf16[64,12,768]{2,1,0:T(8,128)(2,1)} async-done(((bf16[1,12,768]{2,1,0:T(8,128)(2,1)}), bf16[64,12,768]{2,1,0:T(8,128)(2,1)}) %all-gather.27.cloned.1.call-update) | async-done | bytes 1179664 | tf_op jit(solution)/shard_map/all_gather | solution.py:135
  575.8 2.2 reshape.165
  578.1 44.5 %all-gather.17.cloned.1.call-done = bf16[1,4,4,12,64,64]{5,4,3,2,1,0:T(8,128)(2,1)} async-done(((bf16[1,4,4,12,8,64]{5,4,3,2,1,0:T(8,128)(2,1)}), bf16[1,4,4,12,64,64]{5,4,3,2,1,0:T(8,128)(2,1)}) %all-gather.17.cloned.1.call-update) | async-done | bytes 1572880 | tf_op jit(solution)/shard_map/all_gather | solution.py:127
  622.5 4.6 fusion.56
  627.2 37.7 %all-gather.19.cloned.1.call-done = bf16[1,4,4,12,64,64]{5,4,3,2,1,0:T(8,128)(2,1)} async-done(((bf16[1,4,4,12,8,64]{5,4,3,2,1,0:T(8,128)(2,1)}), bf16[1,4,4,12,64,64]{5,4,3,2,1,0:T(8,128)(2,1)}) %all-gather.19.cloned.1.call-update) | async-done | bytes 1572880 | tf_op jit(solution)/shard_map/all_gather | solution.py:128
  664.9 3.1 fusion.24
  670.3 33.1 %all-gather.15.cloned.1.call-done = bf16[1024,768]{1,0:T(8,128)(2,1)} async-done(((bf16[128,768]{1,0:T(8,128)(2,1)}), bf16[1024,768]{1,0:T(8,128)(2,1)}) %all-gather.15.cloned.1.call-update) | async-done | bytes 1572880 | tf_op jit(solution)/shard_map/all_gather | solution.py:141
  703.5 4.6 convolution_convert_fusion.2
  709.5 37.5 %reduce-scatter.2.cloned.1.call-done = bf16[128,768]{1,0:T(8,128)(2,1)} async-done(((bf16[1024,768]{1,0:T(8,128)(2,1)}), bf16[128,768]{1,0:T(8,128)(2,1)}) %reduce-scatter.2.cloned.1.call-update) | async-done | bytes 196624 | tf_op jit(solution)/shard_map/reduce_scatter | solution.py:146
  747.0 1.4 compare_select_fusion
  749.3 13.5 %all-gather.2 = f32[32,4,1]{1,2,0:T(1,128)S(1)} all-gather(f32[4,4,1]{1,2,0:T(1,128)S(1)} %copy.75), channel_id=4, replica_groups=mesh['gx'=64,'gz'=8] {'gz'}, dimensions={0}, use_global_device_ids=true | all-gather | bytes 576 | tf_op jit(solution)/shard_map/all_gather | solution.py:16
  763.8 1.6 fusion.37
  (88 shorter events, 21.4 us)
Async XLA Ops:
  7.2 696.3 %copy-start = (bf16[384,768]{1,0:T(8,128)(2,1)S(1)}, bf16[384,768]{1,0:T(8,128)(2,1)}, u32[]{:S(2)}) copy-start(bf16[384,768]{1,0:T(8,128)(2,1)} %param.18) | copy-start | bytes 1769476
  7.2 146.5 %all-gather.21.cloned.1.call-start = ((), (), s32[]{:S(2)}) async-start(), calls=%async_computation.9 | async-start | bytes 3993600 | tf_op jit(solution)/shard_map/all_gather | solution.py:94
  7.9 285.7 %all-gather.23.cloned.1.call-start = ((), (), s32[]{:S(2)}) async-start(), calls=%async_computation.10 | async-start | bytes 1597440 | tf_op jit(solution)/shard_map/all_gather | solution.py:115
  8.7 430.0 %all-gather.25.cloned.1.call-start = ((), (), s32[]{:S(2)}) async-start(), calls=%async_computation.11 | async-start | bytes 3993600 | tf_op jit(solution)/shard_map/all_gather | solution.py:121
  16.6 4.4 copy-start.4
  16.6 4.6 copy-start.5
  165.2 10.0 %copy-start.3 = (bf16[1,4,8,12,4,64]{5,3,0,2,4,1:T(8,128)(2,1)S(1)}, bf16[1,4,8,12,4,64]{5,3,0,2,4,1:T(8,128)(2,1)}, u32[]{:S(2)}) copy-start(bf16[1,4,8,12,4,64]{5,3,0,2,4,1:T(8,128)(2,1)} %get-tuple-element.128) | copy-start | bytes 589828
  166.5 25.4 %all-to-all-start.1 = ((bf16[64,2,768]{2,1,0:T(2,128)(2,1)}), bf16[64,2,768]{2,1,0:T(2,128)(2,1)S(1)}, u32[]{:S(2)}, u32[]{:S(2)}) async-start(bf16[64,2,768]{2,1,0:T(2,128)(2,1)} %reshape.175), calls=%async_computation.1 | async-start | bytes 393216 | tf_op jit(solution)/shard_map/all_to_all | solution.py:104
  191.9 21.0 %all-to-all-start = ((bf16[64,2,768]{2,1,0:T(2,128)(2,1)}), bf16[64,2,768]{2,1,0:T(2,128)(2,1)S(1)}, u32[]{:S(2)}, u32[]{:S(2)}) async-start(bf16[64,2,768]{2,1,0:T(2,128)(2,1)} %reshape.173), calls=%async_computation | async-start | bytes 393216 | tf_op jit(solution)/shard_map/all_to_all | solution.py:103
  212.9 21.1 %all-to-all-start.2 = ((bf16[64,2,768]{2,1,0:T(2,128)(2,1)}), bf16[64,2,768]{2,1,0:T(2,128)(2,1)S(1)}, u32[]{:S(2)}, u32[]{:S(2)}) async-start(bf16[64,2,768]{2,1,0:T(2,128)(2,1)} %reshape.171), calls=%async_computation.2 | async-start | bytes 393216 | tf_op jit(solution)/shard_map/all_to_all | solution.py:105
  217.5 358.3 %all-gather.27.cloned.1.call-start = ((), (), s32[]{:S(2)}) async-start(), calls=%async_computation.12 | async-start | bytes 1597440 | tf_op jit(solution)/shard_map/all_gather | solution.py:135
  239.2 205.6 %all-to-all-start.3 = ((bf16[64,2,768]{2,1,0:T(2,128)(2,1)}), bf16[64,2,768]{2,1,0:T(2,128)(2,1)S(1)}, u32[]{:S(2)}, u32[]{:S(2)}) async-start(bf16[64,2,768]{2,1,0:T(2,128)(2,1)} %reshape.177), calls=%async_computation.3 | async-start | bytes 393216 | tf_op jit(solution)/shard_map/all_to_all | solution.py:108
  243.9 378.7 %all-gather.17.cloned.1.call-start = ((), (), s32[]{:S(2)}) async-start(), calls=%async_computation.7 | async-start | bytes 3538944 | tf_op jit(solution)/shard_map/all_gather | solution.py:127
  446.2 0.7 copy-start.1
  452.6 212.3 %all-gather.19.cloned.1.call-start = ((), (), s32[]{:S(2)}) async-start(), calls=%async_computation.8 | async-start | bytes 3538944 | tf_op jit(solution)/shard_map/all_gather | solution.py:128
  453.2 250.3 %all-gather.15.cloned.1.call-start = ((), (), s32[]{:S(2)}) async-start(), calls=%async_computation.5 | async-start | bytes 1769472 | tf_op jit(solution)/shard_map/all_gather | solution.py:141
  668.0 1.0 copy-start.2
  670.3 76.7 %reduce-scatter.2.cloned.1.call-start = ((), (), s32[]{:S(2)}) async-start(), calls=%async_computation.6 | async-start | bytes 1769472 | tf_op jit(solution)/shard_map/reduce_scatter | solution.py:146
  708.1 0.7 copy-start.6
Sparse Core Ops, SparseCore 0:
  11.0 142.6 all-gather.20
  156.6 136.9 all-gather.22
  296.6 142.0 all-gather.24
  441.5 134.2 all-gather.26
  577.8 44.7 all-gather.16
  624.5 40.3 all-gather.18
  670.4 33.0 all-gather.14
  708.3 38.6 reduce-scatter.1
where the time goes:
time: 773 us; the launch traced here: 772 us
  waiting for transfers between devices  649 us (84%)
  local copies, waits for them, and re-layouts  41.9 us (5%)
  matrix products  24.7 us (3%)
  starting transfers between devices  23.1 us (3%)
  between operations  15.2 us (2%)
  blocking collectives  13.5 us (2%)
    all_gather x1, waiting for transfers between devices, body(): lax.all_gather(depth_qkv, 'gx', axis=1, tiled=True)  143 us
    all_gather x1, waiting for transfers between devices, body(): lax.all_gather(cross_qkv, 'gx', axis=1, tiled=True)  132 us
    all_gather x1, waiting for transfers between devices, body(): lax.all_gather(depth_out, 'gx', axis=0, tiled=True)  123 us
    all_gather x1, waiting for transfers between devices, body(): lax.all_gather(cross_out, 'gx', axis=0, tiled=True)  49.5 us
    all_gather x1, waiting for transfers between devices, body(): lax.all_gather(lined[1], 'gz', axis=3, tiled=True)  44.5 us
    all_gather x1, waiting for transfers between devices, body(): lax.all_gather(lined[2], 'gz', axis=3, tiled=True)  37.7 us
    reduce_scatter x1, waiting for transfers between devices, body(): lax.psum_scatter(jnp.dot(hidden, down_proj, preferred_element_type=jnp.fl...  37.5 us
    all_gather x1, waiting for transfers between devices, body(): lax.all_gather(normed, 'gz', axis=0, tiled=True)  33.1 us
  transfers between devices with their start and end apart: 12, of which 11 were waited for; matrix products, arithmetic and copies ran while one was open for 7% of the time, Pallas kernels for 0%

commit v1 on v0

v1 whole, which is shorter than its diff:
```python
import functools
import math

import jax
import jax.numpy as jnp
import numpy as np
from jax import lax
from jax.experimental import pallas as pl
from jax.experimental.pallas import tpu as pltpu
from jax.sharding import PartitionSpec as P

ZN, YN, XN = 16, 4, 4
GX, GZ = ZN * YN, XN * 2
D, HEADS, HDIM, FF = 768, 12, 64, 3072
HALF = D // 2
INL, XL, DP = 4, 256, 64
XLD, DPD = XL // GX, DP // GZ
LINES = INL * DPD
MINE = 2 * DP
QKV_ROWS, OUT_ROWS = 144, 48
BLOCK = 2 * (QKV_ROWS + OUT_ROWS)
PIECE = 48
SLOT = 112
MESH = pl.DeviceIdType.MESH
BF, F32 = jnp.bfloat16, jnp.float32
ANY = pl.BlockSpec(memory_space=pl.ANY)
VM = pl.BlockSpec(memory_space=pltpu.VMEM)
LIMIT = 56 << 20


def table():
    k = np.arange(D // 2)
    freq = math.pi * np.exp(-math.log(256.0) * k / (D // 2))
    angle = np.arange(XL)[:, None] * freq[None, :]
    return np.stack([np.sin(angle), np.cos(angle)], -1).reshape(XL, D).astype(np.float32)


def packing():
    one = np.zeros((BLOCK, YN * SLOT), np.float32)
    row = 0
    for at, count in ((0, 36), (40, 12), (56, 36), (96, 12)):
        for y in range(YN):
            for r in range(count):
                one[row, y * SLOT + at + r] = 1
                row += 1
    return one


def place():
    gx, gz = lax.axis_index("gx"), lax.axis_index("gz")
    return gx, gz, gx // YN, gx % YN, gz // 2, gz % 2


def rcopy(src, dst, send, recv, gx, gz):
    return pltpu.make_async_remote_copy(
        src_ref=src, dst_ref=dst, send_sem=send, recv_sem=recv, device_id=(gx, gz), device_id_type=MESH
    )


def signal(gx, gz):
    pl.semaphore_signal(
        pltpu.get_barrier_semaphore(), inc=1, device_id=(gx, gz), device_id_type=MESH
    )


def gather_kernel(
    s_ref, t_ref, col_ref, one_ref, lines, cols, w, ybuf, block,
    y_s, y_r, t_s, t_r, c_s, c_r, z_s, z_r, p_s, p_r, b_s, b_r, l_s,
):
    gx, gz, z, y, x, c = place()
    half = gx // 32
    own_line = half == c
    for d in range(1, 4):
        signal(z * YN + (y + d) % YN, gz)
        signal(gx, ((x + d) % XN) * 2 + c)
    signal(((z + 1) % ZN) * YN + y, gz)
    signal(((z + 15) % ZN) * YN + y, gz)
    for d in range(1, 8):
        signal(gx, (gz + d) % GZ)

    def greet(i, _):
        there = 32 * c + i

        @pl.when(jnp.logical_or(there != gx, half != c))
        def _():
            signal(there, 2 * x + half)

        return 0

    lax.fori_loop(0, 32, greet, 0)
    pl.semaphore_wait(
        pltpu.get_barrier_semaphore(), 15 + 32 - jnp.where(own_line, 1, 0)
    )

    def y_copy(d):
        return rcopy(
            s_ref.at[c], ybuf.at[y], y_s.at[d - 1], y_r.at[d - 1], z * YN + (y + d) % YN, gz
        )

    own_y = pltpu.make_async_copy(s_ref.at[c], ybuf.at[y], l_s.at[0])
    own_y.start()
    for d in range(1, 4):
        y_copy(d).start()

    def t_copy(i):
        return rcopy(t_ref.at[i], lines.at[gx], t_s.at[i], t_r, 32 * c + i, 2 * x + half)

    def t_start(i, _):
        here = jnp.logical_and(32 * c + i == gx, own_line)

        @pl.when(jnp.logical_not(here))
        def _():
            t_copy(i).start()

        @pl.when(here)
        def _():
            pltpu.make_async_copy(t_ref.at[i], lines.at[gx], t_r).start()

        return 0

    lax.fori_loop(0, 32, t_start, 0)

    def c_copy(d):
        there = (gz + d) % GZ
        return rcopy(
            col_ref.at[there], cols.at[gz], c_s.at[d - 1], c_r.at[d - 1], gx, there
        )

    own_c = pltpu.make_async_copy(col_ref.at[gz], cols.at[gz], l_s.at[1])
    own_c.start()
    for d in range(1, 8):
        c_copy(d).start()

    own_y.wait()
    for d in range(1, 4):
        y_copy(d).wait_recv()
    block[...] = jnp.dot(
        one_ref[...], ybuf[...].reshape(YN * SLOT, HALF), preferred_element_type=F32
    ).astype(BF)
    own_w = pltpu.make_async_copy(block, w.at[c, z], l_s.at[2])
    own_w.start()

    rows = (pl.multiple_of(PIECE * y, 16), pl.multiple_of(BLOCK // 2 + PIECE * x, 16))

    def ring(way, s, first=False):
        back = s - 1
        zsrc = (z + jnp.where(way == 0, ZN - back, back)) % ZN
        znext = (z + (1 if way == 0 else ZN - 1)) % ZN
        return [
            rcopy(
                block.at[pl.ds(r, PIECE)] if first else w.at[c, zsrc, pl.ds(r, PIECE)],
                w.at[c, zsrc, pl.ds(r, PIECE)],
                z_s.at[way, s - 1, k],
                z_r.at[way, s - 1, k],
                znext * YN + y,
                gz,
            )
            for k, r in enumerate(rows)
        ]

    def arrived(way, s):
        zsrc = (z + (ZN - s if way == 0 else s)) % ZN
        for k, r in enumerate(rows):
            here = w.at[c, zsrc, pl.ds(r, PIECE)]
            rcopy(here, here, z_s.at[way, s - 1, k], z_r.at[way, s - 1, k], gx, gz).wait_recv()
        return zsrc

    def spread(zsrc):
        out = []
        for d in range(1, 4):
            for k, (tx, tz) in enumerate(
                ((z * YN + (y + d) % YN, gz), (gx, ((x + d) % XN) * 2 + c))
            ):
                piece = w.at[c, zsrc, pl.ds(rows[k], PIECE)]
                n = 2 * (d - 1) + k
                out.append(rcopy(piece, piece, p_s.at[zsrc, n], p_r.at[zsrc, n], tx, tz))
        return out

    def relay(zsrc):
        return rcopy(
            w.at[c, zsrc], w.at[c, zsrc], b_s.at[zsrc], b_r.at[zsrc], gx, 2 * x + 1 - c
        )

    def collect(zsrc):
        for d in range(1, 4):
            for k, r in enumerate(
                (PIECE * ((y + YN - d) % YN), BLOCK // 2 + PIECE * ((x + XN - d) % XN))
            ):
                n = 2 * (d - 1) + k
                here = w.at[c, zsrc, pl.ds(pl.multiple_of(r, 16), PIECE)]
                rcopy(here, here, p_s.at[zsrc, n], p_r.at[zsrc, n], gx, gz).wait_recv()
        relay(zsrc).start()

    for way in range(2):
        for cp in ring(way, 1, True):
            cp.start()
    own_w.wait()
    relay(z).start()

    def l_copy():
        mine = lines.at[pl.ds(pl.multiple_of(32 * c, 32), 32)]
        return rcopy(mine, mine, b_s.at[ZN], b_r.at[ZN], gx, 2 * x + 1 - c)

    def step(s, _):
        zsrc = arrived(0, s)

        @pl.when(s < 8)
        def _():
            for cp in ring(0, s + 1):
                cp.start()

        for cp in spread(zsrc):
            cp.start()

        @pl.when(s < 8)
        def _():
            zsrc = arrived(1, s)

            @pl.when(s < 7)
            def _():
                for cp in ring(1, s + 1):
                    cp.start()

            for cp in spread(zsrc):
                cp.start()

        @pl.when(s > 1)
        def _():
            collect((z + ZN - s + 1) % ZN)
            collect((z + s - 1) % ZN)

        @pl.when(s == 5)
        def _():
            mine = lines.at[pl.ds(pl.multiple_of(32 * c, 32), 32)]
            pltpu.make_async_copy(mine, mine, t_r).wait()
            l_copy().start()

        return 0

    lax.fori_loop(1, 9, step, 0)
    collect((z + 8) % ZN)

    for d in range(1, 8):
        c_copy(d).wait_recv()
        c_copy(d).wait_send()
    own_c.wait()
    for d in range(1, 4):
        y_copy(d).wait_send()

    def t_end(i, _):
        @pl.when(jnp.logical_not(jnp.logical_and(32 * c + i == gx, own_line)))
        def _():
            t_copy(i).wait_send()

        return 0

    lax.fori_loop(0, 32, t_end, 0)
    theirs = lines.at[pl.ds(pl.multiple_of(32 * (1 - c), 32), 32)]
    rcopy(theirs, theirs, b_s.at[ZN], b_r.at[ZN], gx, gz).wait_recv()
    l_copy().wait_send()
    for way in range(2):
        for cp in ring(way, 1, True):
            cp.wait_send()

    def r_end(s, _):
        for cp in ring(0, s):
            cp.wait_send()

        @pl.when(s < 8)
        def _():
            for cp in ring(1, s):
                cp.wait_send()

        return 0

    lax.fori_loop(2, 9, r_end, 0)

    def w_end(k, _):
        zsrc = (z + k) % ZN

        @pl.when(k > 0)
        def _():
            for cp in spread(zsrc):
                cp.wait_send()

        theirs = w.at[1 - c, zsrc]
        rcopy(theirs, theirs, b_s.at[zsrc], b_r.at[zsrc], gx, gz).wait_recv()
        relay(zsrc).wait_send()
        return 0

    lax.fori_loop(0, ZN, w_end, 0)


def gather(shards, lines, cols):
    dma = pltpu.SemaphoreType.DMA
    return pl.pallas_call(
        gather_kernel,
        out_shape=(
            jax.ShapeDtypeStruct((GX, XLD, D), BF),
            jax.ShapeDtypeStruct((GZ, 2 * DPD, D), BF),
            jax.ShapeDtypeStruct((2, ZN, BLOCK, HALF), BF),
        ),
        in_specs=[ANY, ANY, ANY, VM],
        out_specs=(ANY, ANY, ANY),
        scratch_shapes=[
            pltpu.VMEM((YN, SLOT, HALF), BF),
            pltpu.VMEM((BLOCK, HALF), BF),
            dma((3,)), dma((3,)),
            dma((32,)), dma,
            dma((7,)), dma((7,)),
            dma((2, 8, 2)), dma((2, 8, 2)),
            dma((ZN, 6)), dma((ZN, 6)),
            dma((ZN + 1,)), dma((ZN + 1,)),
            dma((3,)),
        ],
        compiler_params=pltpu.CompilerParams(
            collective_id=0, has_side_effects=True, vmem_limit_bytes=LIMIT
        ),
        name="gather",
    )(shards, lines, cols, jnp.asarray(packing(), BF))


def nt(a, b):
    return lax.dot_general(a, b, (((1,), (1,)), ((), ())), preferred_element_type=F32)


def normed(stream, gain):
    scale = lax.rsqrt(jnp.mean(stream * stream, -1, keepdims=True) + 1e-05)
    return (stream * scale * gain).astype(BF)


def which_axis(shape):
    return (lax.broadcasted_iota(jnp.int32, shape, 1) // 2) % 3


def attend(wq, keys_in, queries_in, kbuf, qbuf, vbuf, obuf, mask):
    def project(rows, tokens, left):
        a, b = wq[0, rows, :], wq[1, rows, :]
        lo, hi = tokens[:, :HALF], tokens[:, HALF:]
        return (nt(a, lo) + nt(b, hi) if left else nt(lo, a) + nt(hi, b)).astype(BF)

    qbuf[...] = project(slice(0, D), queries_in, True)
    kbuf[...] = project(slice(D, 2 * D), keys_in, False)
    vbuf[...] = project(slice(2 * D, 3 * D), keys_in, True)
    for h in range(HEADS):
        at = slice(h * HDIM, (h + 1) * HDIM)
        scores = jnp.dot(kbuf[:, at], qbuf[at, :], preferred_element_type=F32) * (HDIM**-0.5)
        if mask is not None:
            scores = jnp.where(mask, scores, -1e30)
        expo = jnp.exp(scores - jnp.max(scores, 0, keepdims=True))
        total = jnp.sum(expo, 0, keepdims=True)
        mixed = jnp.dot(vbuf[at, :], expo.astype(BF), preferred_element_type=F32)
        obuf[at, :] = mixed / total


def line_kernel(tok, enc, gain, w, out, wq, kbuf, qbuf, vbuf, obuf, sem):
    gx, gz, _, _, x, c = place()
    load = pltpu.make_async_copy(w.at[:, :, pl.ds(0, QKV_ROWS), :], wq, sem)
    load.start()
    inl = (gx % 32) // 8
    dep = DPD * (2 * x + gx // 32) + gx % 8
    which = which_axis((XL, D))
    pos = jnp.where(
        which == 1, enc[...], jnp.where(which == 0, enc[pl.ds(inl, 1), :], enc[pl.ds(dep, 1), :])
    )
    n = normed(tok[...].astype(F32) + pos, gain[...])
    q = lax.broadcasted_iota(jnp.int32, (MINE, XL), 0)
    r = lax.broadcasted_iota(jnp.int32, (MINE, XL), 1)
    pick = jnp.where(r == 4 * (q // 2) + 2 * c + q % 2, 1.0, 0.0).astype(BF)
    mine = jnp.dot(pick, n, preferred_element_type=F32).astype(BF)
    load.wait()
    attend(wq.reshape(2, 3 * D, HALF), n, mine, kbuf, qbuf, vbuf, obuf, None)
    out[...] = obuf[...].T.astype(BF)


def line_attention(tok, enc, gain, w):
    return pl.pallas_call(
        line_kernel,
        out_shape=jax.ShapeDtypeStruct((MINE, D), BF),
        in_specs=[VM, VM, VM, ANY],
        out_specs=VM,
        scratch_shapes=[
            pltpu.VMEM((2, ZN, QKV_ROWS, HALF), BF),
            pltpu.VMEM((XL, D), BF),
            pltpu.VMEM((D, MINE), BF),
            pltpu.VMEM((D, XL), BF),
            pltpu.VMEM((D, MINE), F32),
            pltpu.SemaphoreType.DMA,
        ],
        compiler_params=pltpu.CompilerParams(vmem_limit_bytes=LIMIT),
        name="line_attention",
    )(tok, enc, gain, w)


def back_kernel(mixed, out, s_sem, r_sem):
    gx, gz, _, _, x, c = place()
    inl = (gx % 32) // 8
    dep = DPD * (2 * x + gx // 32) + gx % 8
    me_too = inl == x

    def greet(i, _):
        there, other = 32 * ((i // 8) % 2) + 8 * x + i % 8, 2 * (i // 16) + c

        @pl.when(jnp.logical_or(there != gx, other != gz))
        def _():
            signal(there, other)

        return 0

    lax.fori_loop(0, 64, greet, 0)
    pl.semaphore_wait(pltpu.get_barrier_semaphore(), 64 - jnp.where(me_too, 1, 0))

    def copy(i):
        return rcopy(mixed.at[i], out.at[dep], s_sem.at[i], r_sem, i, 2 * inl + c)

    def start(i, _):
        here = jnp.logical_and(i == gx, me_too)

        @pl.when(jnp.logical_not(here))
        def _():
            copy(i).start()

        @pl.when(here)
        def _():
            pltpu.make_async_copy(mixed.at[i], out.at[dep], r_sem).start()

        return 0

    lax.fori_loop(0, 64, start, 0)
    pltpu.make_async_copy(out, out, r_sem).wait()

    def end(i, _):
        @pl.when(jnp.logical_not(jnp.logical_and(i == gx, me_too)))
        def _():
            copy(i).wait_send()

        return 0

    lax.fori_loop(0, 64, end, 0)


def back(mixed):
    return pl.pallas_call(
        back_kernel,
        out_shape=jax.ShapeDtypeStruct((DP, 2, D), BF),
        in_specs=[ANY],
        out_specs=ANY,
        scratch_shapes=[pltpu.SemaphoreType.DMA((64,)), pltpu.SemaphoreType.DMA],
        compiler_params=pltpu.CompilerParams(collective_id=1, has_side_effects=True),
        name="back",
    )(mixed)


def column_kernel(
    mixed, cols, enc, dep2, gains, w, stream_out, normed_out,
    w2, wq, w4, kbuf, qbuf, vbuf, obuf, sem,
):
    gx, _, _, _, x, c = place()
    parts = (0, QKV_ROWS), (QKV_ROWS, OUT_ROWS), (BLOCK // 2, QKV_ROWS), (BLOCK // 2 + QKV_ROWS, OUT_ROWS)
    loads = [
        pltpu.make_async_copy(w.at[:, :, pl.ds(*parts[k]), :], to, sem.at[k - 1])
        for k, to in ((1, w2), (2, wq), (3, w4))
    ]
    for load in loads:
        load.start()
    which = which_axis((MINE, D))
    odd = lax.broadcasted_iota(jnp.int32, (MINE, D), 0) % 2
    first = XLD * gx + 2 * c
    cross = jnp.where(odd == 0, enc[pl.ds(first, 1), :], enc[pl.ds(first + 1, 1), :])
    pos = jnp.where(which == 1, cross, jnp.where(which == 0, enc[pl.ds(x, 1), :], dep2[...]))
    stream = cols[...].astype(F32) + pos

    def project(v, wo):
        return jnp.concatenate(
            [
                jnp.dot(v, wo[k].reshape(D, HALF), preferred_element_type=F32)
                for k in range(2)
            ],
            1,
        )

    loads[0].wait()
    stream = stream + project(mixed[...], w2)
    n = normed(stream, gains[1:2, :])
    mask = (
        lax.broadcasted_iota(jnp.int32, (MINE, MINE), 0)
        + lax.broadcasted_iota(jnp.int32, (MINE, MINE), 1)
    ) % 2 == 0
    loads[1].wait()
    attend(wq.reshape(2, 3 * D, HALF), n, n, kbuf, qbuf, vbuf, obuf, mask)
    loads[2].wait()
    stream = stream + project(obuf[...].T.astype(BF), w4)
    stream_out[...] = stream
    normed_out[...] = normed(stream, gains[2:3, :])


def column_attention(mixed, cols, enc, dep2, gains, w):
    return pl.pallas_call(
        column_kernel,
        out_shape=(
            jax.ShapeDtypeStruct((MINE, D), F32),
            jax.ShapeDtypeStruct((MINE, D), BF),
        ),
        in_specs=[VM, VM, VM, VM, VM, ANY],
        out_specs=(VM, VM),
        scratch_shapes=[
            pltpu.VMEM((2, ZN, OUT_ROWS, HALF), BF),
            pltpu.VMEM((2, ZN, QKV_ROWS, HALF), BF),
            pltpu.VMEM((2, ZN, OUT_ROWS, HALF), BF),
            pltpu.VMEM((MINE, D), BF),
            pltpu.VMEM((D, MINE), BF),
            pltpu.VMEM((D, MINE), BF),
            pltpu.VMEM((D, MINE), F32),
            pltpu.SemaphoreType.DMA((3,)),
        ],
        compiler_params=pltpu.CompilerParams(vmem_limit_bytes=LIMIT),
        name="column_attention",
    )(mixed, cols, enc, dep2, gains, w)


def mlp_kernel(
    n_ref, stream, up, down, head_w, head_b, feat, time,
    tokens, sent, pair, sums, got, fbuf, gbuf,
    g_s, g_r, b_s, b_r, q_s, q_r, s_s, s_r, f_s, f_r, h_s, h_r, l_s,
):
    gx, gz, _, _, x, c = place()
    sib = 2 * x + 1 - c
    for d in range(1, 8):
        signal(gx, (gz + d) % GZ)
    pl.semaphore_wait(pltpu.get_barrier_semaphore(), 7)

    def to_chip(d):
        return rcopy(n_ref, tokens.at[d, c], g_s.at[d - 1], g_r.at[d - 1], gx, ((x + d) % XN) * 2 + c)

    def to_sib(d):
        src = n_ref if d == 0 else tokens.at[d, c]
        return rcopy(src, tokens.at[d, c], b_s.at[d], b_r.at[d], gx, sib)

    order = (1, 3, 2)
    for d in order:
        to_chip(d).start()
    to_sib(0).start()
    own = pltpu.make_async_copy(n_ref, tokens.at[0, c], l_s.at[0])
    own.start()

    def from_sib(d):
        here = tokens.at[d, 1 - c]
        return rcopy(here, here, b_s.at[d], b_r.at[d], gx, sib)

    def pair_copy(d):
        return rcopy(sent.at[d, 1 - c], pair.at[d], q_s.at[d], q_r.at[d], gx, sib)

    def home(d):
        return rcopy(
            sums.at[d], got.at[d - 1], s_s.at[d - 1], s_r.at[d - 1], gx, ((x + XN - d) % XN) * 2 + c
        )

    def finish(d):
        pair_copy(d).wait_recv()
        both = sent[d, c].astype(F32) + pair[d].astype(F32)
        if d == 0:
            return both
        sums[d] = both.astype(BF)
        home(d).start()
        return None

    def hidden_part(d):
        rows = tokens[d].reshape(2 * MINE, D)
        hidden = jax.nn.gelu(jnp.dot(rows, up[...], preferred_element_type=F32)).astype(BF)
        part = jnp.dot(hidden, down[...], preferred_element_type=F32).astype(BF)
        sent[d] = part.reshape(2, MINE, D)
        pair_copy(d).start()

    own.wait()
    from_sib(0).wait_recv()
    hidden_part(0)
    last = 0
    for d in order:
        to_chip(d).wait_recv()
        to_sib(d).start()
        from_sib(d).wait_recv()
        hidden_part(d)
        if last:
            finish(last)
        last = d
    finish(last)
    total = finish(0)
    for d in order:
        home(d).wait_recv()
        total = total + got[d - 1].astype(F32)
    stream3 = stream[...] + total
    fbuf[...] = stream3.astype(BF)
    thick = jax.nn.softplus(jnp.sum(stream3 * head_w[...], -1, keepdims=True) + head_b[0, 0])
    i = lax.broadcasted_iota(jnp.int32, (MINE, MINE), 0)
    j = lax.broadcasted_iota(jnp.int32, (MINE, MINE), 1)
    keep = jnp.logical_and(i <= j, (i + j) % 2 == 0)
    line = jnp.sum(jnp.where(keep, thick, 0.0), 0, keepdims=True)
    gbuf[...] = jnp.broadcast_to(line, (8, MINE))

    def f_copy(d):
        there = (gz + d) % GZ
        rows = fbuf.at[pl.ds(pl.multiple_of(16 * there, 16), 16)]
        return rcopy(rows, feat.at[gz], f_s.at[d - 1], f_r.at[d - 1], gx, there)

    def h_copy(d):
        return rcopy(gbuf, time.at[gz], h_s.at[d - 1], h_r.at[d - 1], gx, (gz + d) % GZ)

    for d in range(1, 8):
        f_copy(d).start()
        h_copy(d).start()
    own_f = pltpu.make_async_copy(fbuf.at[pl.ds(pl.multiple_of(16 * gz, 16), 16)], feat.at[gz], l_s.at[1])
    own_h = pltpu.make_async_copy(gbuf, time.at[gz], l_s.at[2])
    own_f.start()
    own_h.start()
    for d in range(1, 8):
        f_copy(d).wait()
        h_copy(d).wait()
    own_f.wait()
    own_h.wait()
    for d in range(1, 4):
        to_chip(d).wait_send()
        home(d).wait_send()
    for d in range(4):
        to_sib(d).wait_send()
        pair_copy(d).wait_send()


def mlp(n, stream, up, down, head_w, head_b):
    dma = pltpu.SemaphoreType.DMA
    return pl.pallas_call(
        mlp_kernel,
        out_shape=(
            jax.ShapeDtypeStruct((GZ, 16, D), BF),
            jax.ShapeDtypeStruct((GZ, 8, MINE), F32),
        ),
        in_specs=[VM, VM, VM, VM, VM, pl.BlockSpec(memory_space=pltpu.SMEM)],
        out_specs=(ANY, ANY),
        scratch_shapes=[
            pltpu.VMEM((4, 2, MINE, D), BF),
            pltpu.VMEM((4, 2, MINE, D), BF),
            pltpu.VMEM((4, MINE, D), BF),
            pltpu.VMEM((4, MINE, D), BF),
            pltpu.VMEM((3, MINE, D), BF),
            pltpu.VMEM((MINE, D), BF),
            pltpu.VMEM((8, MINE), F32),
            dma((3,)), dma((3,)),
            dma((4,)), dma((4,)),
            dma((4,)), dma((4,)),
            dma((3,)), dma((3,)),
            dma((7,)), dma((7,)),
            dma((7,)), dma((7,)),
            dma((3,)),
        ],
        compiler_params=pltpu.CompilerParams(
            collective_id=2, has_side_effects=True, vmem_limit_bytes=LIMIT
        ),
        name="mlp",
    )(n, stream, up, down, head_w, head_b)


def body(
    tokens, cross_qkv, cross_out, depth_qkv, depth_out, up_proj, down_proj, gains, head_weight, head_bias
):
    gz = lax.axis_index("gz")
    enc = table()
    dep2 = jnp.asarray(np.repeat(enc[:DP], 2, 0))
    enc = jnp.asarray(enc)

    def pad(a, rows):
        return jnp.pad(a, ((0, rows - a.shape[0]), (0, 0)))

    shard = jnp.concatenate(
        [pad(cross_qkv.T, 40), pad(cross_out, 16), pad(depth_qkv.T, 40), pad(depth_out, 16)]
    )
    shard = jnp.stack([shard[:, :HALF], shard[:, HALF:]])
    by_line = jnp.transpose(tokens, (0, 2, 1, 3)).reshape(LINES, XLD, D)
    by_column = tokens.reshape(GZ, 2, DPD, D)
    by_column = jnp.transpose(by_column, (0, 2, 1, 3)).reshape(GZ, 2 * DPD, D)
    lines, cols, w = gather(shard, by_line, by_column)
    mixed = line_attention(lines.reshape(XL, D), enc, gains[0:1], w)
    mixed = back(mixed.reshape(GX, 2, D))
    stream, n = column_attention(
        mixed.reshape(MINE, D), cols.reshape(MINE, D), enc, dep2, gains, w
    )
    feat, time = mlp(n, stream, up_proj, down_proj, head_weight[None], head_bias[None])
    feat = jnp.transpose(feat.reshape(INL, 2, DPD, 2, D), (0, 1, 3, 2, 4))
    feat = feat.reshape(INL, XLD, DPD, D)
    time = lax.dynamic_slice_in_dim(time[:, 0, :], 16 * gz, 16, 1)
    time = jnp.transpose(time.reshape(INL, 2, DPD, 2), (0, 1, 3, 2)).reshape(INL, XLD, DPD)
    return feat, time


def solution(mesh):
    return jax.shard_map(
        body,
        mesh=mesh,
        in_specs=(
            P(None, "gx", "gz", None),
            P(None, "gx"),
            P("gx", None),
            P(None, "gx"),
            P("gx", None),
            P(None, "gz"),
            P("gz", None),
            P(),
            P(),
            P(),
        ),
        out_specs=(P(None, "gx", "gz", None), P(None, "gx", "gz")),
        check_vma=False,
    )
```

time: 773 us -> 155 us (0.20)
  waiting for transfers between devices: 649 us -> 0 us
  Pallas kernels: 0 us -> 137 us
  local copies, waits for them, and re-layouts: 41.9 us -> 14 us
  matrix products: 24.7 us -> 0 us
  starting transfers between devices: 23.1 us -> 0 us
  between operations: 15.2 us -> 1.36 us
  blocking collectives: 13.5 us -> 0 us
    all_gather x7 -> x0, waiting for transfers between devices: 563 us -> none  [the longest x1 143 us: body(): lax.all_gather(depth_qkv, 'gx', axis=1, tiled=True)]
    pallas_call x0 -> x5, Pallas kernels: none -> 137 us  [the longest x1 69 us: gather(): pl.pallas_call(gather_kernel, out_shape=(jax.ShapeDtypeStruct((GX, XLD, D...]
    all_to_all x4 -> x0, waiting for transfers between devices: 45.6 us -> none  [the longest x1 15.4 us: body(): lax.all_to_all(lined[1], 'gx', split_axis=0, concat_axis=2, tiled=True)]
    reduce_scatter x1 -> x0, waiting for transfers between devices: 37.5 us -> none  [body(): lax.psum_scatter(jnp.dot(hidden, down_proj, preferred_element_type=jnp.fl...]
    unnamed x27 -> x2, local copies, waits for them, and re-layouts: 23.7 us -> 0.01 us
    all_to_all x4 -> x0, starting transfers between devices: 22.6 us -> none  [the longest x1 8.72 us: body(): lax.all_to_all(lined[1], 'gx', split_axis=0, concat_axis=2, tiled=True)]
    dot_general x8 -> x0, matrix products: 18.2 us -> none  [the longest x2 4.8 us: attend(): jnp.einsum('...qk,...ke->...qe', weights, values, preferred_element_type=...]
    all_gather x1 -> x0, blocking collectives: 13.5 us -> none  [carried_in(): everything = lax.all_gather(shard, axis)]
  transfers between devices with their start and end apart: 12 -> 0, of which waited for: 11 -> 0; matrix products, arithmetic and copies ran while one was open for 7% -> 0% of each run, Pallas kernels for 0% -> 0%
where the time goes in v1:
time: 155 us; the launch traced here: 154 us
  Pallas kernels  137 us (88%)
  local copies, waits for them, and re-layouts  14 us (9%)
  other arithmetic  1.6 us (1%)
    pallas_call x1, Pallas kernels, gather(): pl.pallas_call(gather_kernel, out_shape=(jax.ShapeDtypeStruct((GX, XLD, D...  69 us
    pallas_call x1, Pallas kernels, mlp(): pl.pallas_call(mlp_kernel, out_shape=(jax.ShapeDtypeStruct((GZ, 16, D), B...  34.6 us
    pallas_call x1, Pallas kernels, back(): pl.pallas_call(back_kernel, out_shape=jax.ShapeDtypeStruct((DP, 2, D), BF...  19.2 us
    pallas_call x1, Pallas kernels, line_attention(): pl.pallas_call(line_kernel, out_shape=jax.ShapeDtypeStruct((MINE, D), BF)...  7.88 us
    pallas_call x1, Pallas kernels, column_attention(): pl.pallas_call(column_kernel, out_shape=(jax.ShapeDtypeStruct((MINE, D),...  6.55 us

profile of v1, /device:TPU:1, one launch (start us, length us, event | category | flops | bytes accessed | tf_op | source)
XLA Modules:
  0.0 154.1 jit_solution(1621089509861410900)
XLA Ops:
  0.6 0.9 fusion.7
  1.6 0.7 pad_maximum_fusion.s_ref
  2.3 1.1 copy.24
  3.3 0.7 reshape.41.col_ref
  4.1 1.7 %copy.19 = bf16[4,8,4,768]{3,2,1,0:T(4,128)(2,1)} copy(bf16[4,8,4,768]{3,1,2,0:T(8,128)(2,1)} %bitcast.20) | data formatting | bytes 393216 | tf_op jit(solution)/shard_map/transpose | solution.py:676
  5.8 69.0 %gather.1 = (bf16[64,4,768]{2,1,0:T(4,128)(2,1)}, bf16[8,16,768]{2,1,0:T(8,128)(2,1)}, bf16[2,16,384,384]{3,2,1,0:T(8,128)(2,1)}) custom-call(bf16[2,112,384]{2,1,0:T(8,128)(2,1)} %pad_maximum_fusion.s_ref, bf16[32,4,768]{2,1,0:T(4,128)(2,1)} %bitcast.23, bf16[8,16,768]{2,1,0:T(8,128)(2,1)} %reshape.41.col_ref, bf16[384,448]{1,0:T(8,128)(2,1)} %constant.21.clone.one_ref), custom_call_target="tpu_custom_call" | custom-call | tf_op jit(solution)/shard_map/gather/pallas_call | solution.py:296
  74.7 1.9 %reshape.42.tok = bf16[256,768]{1,0:T(8,128)(2,1)} reshape(bf16[64,4,768]{2,1,0:T(4,128)(2,1)} %get-tuple-element.9) | data formatting | bytes 786432 | tf_op jit(solution)/shard_map/reshape | solution.py:680
  76.6 1.3 slice.14.gain
  77.9 0.0 copy-start
  77.9 7.9 %line_attention.1 = bf16[128,768]{1,0:T(8,128)(2,1)} custom-call(bf16[256,768]{1,0:T(8,128)(2,1)} %reshape.42.tok, f32[256,768]{1,0:T(8,128)} %constant.20.clone.enc, f32[1,768]{1,0:T(1,128)} %slice.14.gain, bf16[2,16,384,384]{3,2,1,0:T(8,128)(2,1)} %get-tuple-element.10.w), custom_call_target="tpu_custom_call" | custom-call | tf_op jit(solution)/shard_map/line_attention/pallas_call | solution.py:377
  85.8 1.7 %reshape.43.mixed = bf16[64,2,768]{2,1,0:T(2,128)(2,1)} reshape(bf16[128,768]{1,0:T(8,128)(2,1)} %line_attention.1) | data formatting | bytes 393216 | tf_op jit(solution)/shard_map/reshape | solution.py:681
  87.5 19.2 %back.1 = bf16[64,2,768]{2,1,0:T(2,128)(2,1)} custom-call(bf16[64,2,768]{2,1,0:T(2,128)(2,1)} %reshape.43.mixed), custom_call_target="tpu_custom_call" | custom-call | tf_op jit(solution)/shard_map/back/pallas_call | solution.py:443
  106.7 1.7 %reshape.44.mixed = bf16[128,768]{1,0:T(8,128)(2,1)} reshape(bf16[64,2,768]{2,1,0:T(2,128)(2,1)} %back.1) | data formatting | bytes 393216 | tf_op jit(solution)/shard_map/reshape | solution.py:683
  108.4 6.6 %column_attention.1 = (f32[128,768]{1,0:T(8,128)}, bf16[128,768]{1,0:T(8,128)(2,1)}) custom-call(bf16[128,768]{1,0:T(8,128)(2,1)} %reshape.44.mixed, bf16[128,768]{1,0:T(8,128)(2,1)} %bitcast.25, f32[256,768]{1,0:T(8,128)} %constant.20.clone.enc, f32[128,768]{1,0:T(8,128)} %constant.19.clone.dep2, f32[3,768]{1,0:T(4,128)} %gains.1, ...), custom_call_target="tpu_custom_call" | custom-call | tf_op jit(solution)/shard_map/column_attention/pallas_call | solution.py:498
  114.9 0.0 copy-done
  114.9 0.6 broadcast_in_dim.6.head_w
  116.2 34.6 %mlp.1 = (bf16[8,16,768]{2,1,0:T(8,128)(2,1)}, f32[8,8,128]{2,1,0:T(8,128)}) custom-call(bf16[128,768]{1,0:T(8,128)(2,1)} %get-tuple-element.12.n_ref, f32[128,768]{1,0:T(8,128)} %get-tuple-element.13.stream, bf16[768,384]{1,0:T(8,128)(2,1)} %up.1, bf16[384,768]{1,0:T(8,128)(2,1)} %down.1, f32[1,768]{1,0:T(1,128)} %broadcast_in_dim.6.head_w, ...), custom_call_target="tpu_custom_call" | custom-call | tf_op jit(solution)/shard_map/mlp/pallas_call | solution.py:630
  150.8 0.8 slice.15
  151.5 0.1 dynamic-slice_reduce_fusion
  151.6 0.1 reshape.48
  151.7 0.7 copy.22
  152.4 1.0 reshape.46
  153.4 0.7 copy.21
  (1 shorter events, 0.0 us)
Async XLA Ops:
  77.9 37.0 %copy-start = (f32[768]{0:T(1024)S(1)}, f32[768]{0:T(1024)}, u32[]{:S(2)}) copy-start(f32[768]{0:T(1024)} %param.21) | copy-start | bytes 9220

commit v2 on v0

v2 whole, which is shorter than its diff:
```python
import functools
import math

import jax
import jax.numpy as jnp
import numpy as np
from jax import lax
from jax.experimental import pallas as pl
from jax.experimental.pallas import tpu as pltpu
from jax.sharding import PartitionSpec as P

ZN, YN, XN = 16, 4, 4
GX, GZ = ZN * YN, XN * 2
D, HEADS, HDIM, FF = 768, 12, 64, 3072
HALF = D // 2
INL, XL, DP = 4, 256, 64
XLD, DPD = XL // GX, DP // GZ
LINES = INL * DPD
MINE = 2 * DP
QKV_ROWS, OUT_ROWS = 144, 48
KIND = QKV_ROWS + OUT_ROWS
BLOCK = 2 * KIND
QKV, SPAN = 3 * D, 4 * D
PIECE = 48
SLOT = 112
MESH = pl.DeviceIdType.MESH
BF, F32 = jnp.bfloat16, jnp.float32
ANY = pl.BlockSpec(memory_space=pl.ANY)
VM = pl.BlockSpec(memory_space=pltpu.VMEM)
LIMIT = 56 << 20


def table():
    k = np.arange(D // 2)
    freq = math.pi * np.exp(-math.log(256.0) * k / (D // 2))
    angle = np.arange(XL)[:, None] * freq[None, :]
    return np.stack([np.sin(angle), np.cos(angle)], -1).reshape(XL, D).astype(np.float32)


def packing():
    one = np.zeros((BLOCK, YN * SLOT), np.float32)
    row = 0
    for at, count in ((0, 36), (40, 12), (56, 36), (96, 12)):
        for y in range(YN):
            for r in range(count):
                one[row, y * SLOT + at + r] = 1
                row += 1
    return one


def place():
    gx, gz = lax.axis_index("gx"), lax.axis_index("gz")
    return gx, gz, gx // YN, gx % YN, gz // 2, gz % 2


def rcopy(src, dst, send, recv, gx, gz):
    return pltpu.make_async_remote_copy(
        src_ref=src, dst_ref=dst, send_sem=send, recv_sem=recv, device_id=(gx, gz), device_id_type=MESH
    )


def signal(gx, gz):
    pl.semaphore_signal(
        pltpu.get_barrier_semaphore(), inc=1, device_id=(gx, gz), device_id_type=MESH
    )


def nt(a, b):
    return lax.dot_general(a, b, (((1,), (1,)), ((), ())), preferred_element_type=F32)


def normed(stream, gain):
    scale = lax.rsqrt(jnp.mean(stream * stream, -1, keepdims=True) + 1e-05)
    return (stream * scale * gain).astype(BF)


def which_axis(shape):
    return (lax.broadcasted_iota(jnp.int32, shape, 1) // 2) % 3


def rows16(start, size):
    return pl.ds(pl.multiple_of(start, 16), size)


def block_kernel(
    tok, w1, w2, w3, w4, gains, head_w, head_b, one_ref, enc_h, dep2_h, up_h, down_h,
    feat, time,
    enc, dep2, up, down, sbuf, shard, ybuf, block, w, by_line, lines, cols, nbuf,
    kbuf, qbuf, vbuf, obuf, sendb, mixed, nown, tokens, sent, pair, sums, got, stage, fbuf, gbuf, frecv, trecv,
    y_s, y_r, t_s, t_r, c_s, c_r, z_s, z_r, p_s, p_r, b_s, b_r, i_s, i_r, k_s, k_r,
    g_s, g_r, a_s, a_r, q_s, q_r, s_s, s_r, f_s, f_r, h_s, h_r, l_s,
):
    gx, gz, z, y, x, c = place()
    half = gx // 32
    own_line = half == c
    sib = 2 * x + 1 - c
    inl = (gx % 32) // 8
    dep = DPD * (2 * x + half) + gx % 8
    me_too = inl == x

    def greet_lines(i, _):
        there = 32 * c + i

        @pl.when(jnp.logical_or(there != gx, half != c))
        def _():
            signal(there, 2 * x + half)

        return 0

    lax.fori_loop(0, 32, greet_lines, 0)

    def greet_back(i, _):
        there, other = 32 * ((i // 8) % 2) + 8 * x + i % 8, 2 * (i // 16) + c

        @pl.when(jnp.logical_or(there != gx, other != gz))
        def _():
            signal(there, other)

        return 0

    lax.fori_loop(0, 64, greet_back, 0)
    for d in range(1, 4):
        signal(z * YN + (y + d) % YN, gz)
    signal(((z + 1) % ZN) * YN + y, gz)
    signal(((z + 15) % ZN) * YN + y, gz)
    for d in range(1, 8):
        signal(gx, (gz + d) % GZ)

    loads = [
        pltpu.make_async_copy(a, b, l_s.at[k])
        for k, (a, b) in enumerate(((enc_h, enc), (dep2_h, dep2), (up_h, up), (down_h, down)))
    ]
    for load in loads:
        load.start()
    sbuf[...] = jnp.zeros_like(sbuf)
    sbuf[0:36, :] = w1[...].astype(F32).T
    sbuf[40:52, :] = w2[...].astype(F32)
    sbuf[56:92, :] = w3[...].astype(F32).T
    sbuf[96:108, :] = w4[...].astype(F32)
    shard[0] = sbuf[:, :HALF].astype(BF)
    shard[1] = sbuf[:, HALF:].astype(BF)
    by_line[...] = (
        jnp.transpose(tok[...].astype(F32), (0, 2, 1, 3)).reshape(LINES, XLD, D).astype(BF)
    )
    pl.semaphore_wait(
        pltpu.get_barrier_semaphore(),
        12 + 32 + 64 - jnp.where(own_line, 1, 0) - jnp.where(me_too, 1, 0),
    )

    def y_copy(d):
        return rcopy(
            shard.at[c], ybuf.at[y], y_s.at[d - 1], y_r.at[d - 1], z * YN + (y + d) % YN, gz
        )

    own_y = pltpu.make_async_copy(shard.at[c], ybuf.at[y], l_s.at[4])
    own_y.start()
    for d in (1, 3, 2):
        y_copy(d).start()

    def t_copy(i):
        return rcopy(by_line.at[i], lines.at[gx], t_s.at[i], t_r, 32 * c + i, 2 * x + half)

    def t_start(i, _):
        here = jnp.logical_and(32 * c + i == gx, own_line)

        @pl.when(jnp.logical_not(here))
        def _():
            t_copy(i).start()

        @pl.when(here)
        def _():
            pltpu.make_async_copy(by_line.at[i], lines.at[gx], t_r).start()

        return 0

    lax.fori_loop(0, 32, t_start, 0)

    def c_copy(d):
        there = (gz + d) % GZ
        return rcopy(
            tok.at[there // 2, pl.ds(2 * (there % 2), 2)], cols.at[gz], c_s.at[d - 1], c_r.at[d - 1], gx, there
        )

    own_c = pltpu.make_async_copy(tok.at[x, pl.ds(2 * c, 2)], cols.at[gz], l_s.at[5])
    own_c.start()
    for d in range(1, 8):
        c_copy(d).start()

    own_y.wait()
    for d in range(1, 4):
        y_copy(d).wait_recv()
    block[...] = jnp.dot(
        one_ref[...], ybuf[...].reshape(YN * SLOT, HALF), preferred_element_type=F32
    ).astype(BF)

    def who(kind):
        return x if kind else y

    def near(kind, d):
        if kind:
            return gx, ((x + d) % XN) * 2 + c
        return z * YN + (y + d) % YN, gz

    def piece(kind, zsrc, k):
        at = SPAN * kind + jnp.where(k < 3, QKV_ROWS * zsrc + PIECE * k, QKV + PIECE * zsrc)
        return w.at[c, rows16(at, PIECE)]

    def parts(kind, zsrc, core):
        return (
            w.at[core, rows16(SPAN * kind + QKV_ROWS * zsrc, QKV_ROWS)],
            w.at[core, rows16(SPAN * kind + QKV + OUT_ROWS * zsrc, OUT_ROWS)],
        )

    own_parts = [
        pltpu.make_async_copy(
            block.at[pl.ds(KIND * kind + (0, QKV_ROWS)[k], (QKV_ROWS, OUT_ROWS)[k])],
            parts(kind, z, c)[k],
            l_s.at[6 + 2 * kind + k],
        )
        for kind in range(2)
        for k in range(2)
    ]
    for cp in own_parts:
        cp.start()

    def ring(kind, way, s, first=False):
        back = s - 1
        zsrc = (z + (ZN - back if way == 0 else back)) % ZN
        znext = (z + (1 if way == 0 else ZN - 1)) % ZN
        to = piece(kind, zsrc, who(kind))
        src = block.at[rows16(KIND * kind + PIECE * who(kind), PIECE)] if first else to
        return rcopy(
            src, to, z_s.at[kind, way, s - 1], z_r.at[kind, way, s - 1], znext * YN + y, gz
        )

    def arrived(kind, way, s):
        zsrc = (z + (ZN - s if way == 0 else s)) % ZN
        here = piece(kind, zsrc, who(kind))
        rcopy(here, here, z_s.at[kind, way, s - 1], z_r.at[kind, way, s - 1], gx, gz).wait_recv()
        return zsrc

    def spread(kind, zsrc):
        mine = piece(kind, zsrc, who(kind))
        return [
            rcopy(mine, mine, p_s.at[kind, zsrc, n], p_r.at[kind, zsrc, n], *near(kind, d))
            for n, d in enumerate((1, 3))
        ]

    def onward(kind, zsrc):
        odd = zsrc % 2
        it = piece(kind, zsrc, (who(kind) + jnp.where(odd == 0, 3, 1)) % 4)
        return rcopy(
            it, it, p_s.at[kind, zsrc, 2], p_r.at[kind, zsrc, 2], *near(kind, jnp.where(odd == 0, 1, 3))
        )

    def relay(kind, zsrc):
        return [
            rcopy(a, a, b_s.at[kind, zsrc, k], b_r.at[kind, zsrc, k], gx, sib)
            for k, a in enumerate(parts(kind, zsrc, c))
        ]

    def collect_near(kind, zsrc):
        for n, d in enumerate((3, 1)):
            here = piece(kind, zsrc, (who(kind) + d) % 4)
            rcopy(here, here, p_s.at[kind, zsrc, n], p_r.at[kind, zsrc, n], gx, gz).wait_recv()
        onward(kind, zsrc).start()

    def collect_far(kind, zsrc):
        here = piece(kind, zsrc, (who(kind) + 2) % 4)
        rcopy(here, here, p_s.at[kind, zsrc, 2], p_r.at[kind, zsrc, 2], gx, gz).wait_recv()
        for cp in relay(kind, zsrc):
            cp.start()

    def begin(kind):
        for way in range(2):
            ring(kind, way, 1, True).start()
        for cp in own_parts[2 * kind : 2 * kind + 2]:
            cp.wait()
        for cp in relay(kind, z):
            cp.start()

    def step(kind, s):
        @pl.when(s <= 8)
        def _():
            zsrc = arrived(kind, 0, s)

            @pl.when(s < 8)
            def _():
                ring(kind, 0, s + 1).start()

            for cp in spread(kind, zsrc):
                cp.start()

        @pl.when(s <= 7)
        def _():
            zsrc = arrived(kind, 1, s)

            @pl.when(s < 7)
            def _():
                ring(kind, 1, s + 1).start()

            for cp in spread(kind, zsrc):
                cp.start()

        @pl.when(jnp.logical_and(s >= 2, s <= 9))
        def _():
            collect_near(kind, (z + ZN - s + 1) % ZN)

        @pl.when(jnp.logical_and(s >= 2, s <= 8))
        def _():
            collect_near(kind, (z + s - 1) % ZN)

        @pl.when(jnp.logical_and(s >= 3, s <= 10))
        def _():
            collect_far(kind, (z + ZN - s + 2) % ZN)

        @pl.when(jnp.logical_and(s >= 3, s <= 9))
        def _():
            collect_far(kind, (z + s - 2) % ZN)

    def siblings(kind):
        def one(zsrc, _):
            for k, a in enumerate(parts(kind, zsrc, 1 - c)):
                rcopy(a, a, b_s.at[kind, zsrc, k], b_r.at[kind, zsrc, k], gx, gz).wait_recv()
            return 0

        lax.fori_loop(0, ZN, one, 0)

    def l_copy():
        mine = lines.at[rows16(32 * c, 32)]
        return rcopy(mine, mine, i_s, i_r, gx, sib)

    begin(0)

    def cross_step(s, _):
        step(0, s)

        @pl.when(s == 6)
        def _():
            mine = lines.at[rows16(32 * c, 32)]
            pltpu.make_async_copy(mine, mine, t_r).wait()
            l_copy().start()

        return 0

    lax.fori_loop(1, 9, cross_step, 0)
    begin(1)
    lax.fori_loop(9, 11, cross_step, 0)

    loads[0].wait()
    loads[1].wait()
    theirs = lines.at[rows16(32 * (1 - c), 32)]
    rcopy(theirs, theirs, i_s, i_r, gx, gz).wait_recv()
    which = which_axis((XL, D))
    pos = jnp.where(
        which == 1, enc[...], jnp.where(which == 0, enc[pl.ds(inl, 1), :], enc[pl.ds(dep, 1), :])
    )
    nbuf[...] = normed(lines[...].astype(F32).reshape(XL, D) + pos, gains[0:1, :])
    q = lax.broadcasted_iota(jnp.int32, (MINE, XL), 0)
    r = lax.broadcasted_iota(jnp.int32, (MINE, XL), 1)
    pick = jnp.where(r == 4 * (q // 2) + 2 * c + q % 2, 1.0, 0.0).astype(BF)
    nown[...] = jnp.dot(pick, nbuf[...], preferred_element_type=F32).astype(BF)

    def attend(base, keys_in, queries_in, count, mask, between):
        def project(part, tokens_in, left):
            a, b = (w[k, base + part * D : base + (part + 1) * D, :] for k in range(2))
            lo, hi = tokens_in[:, :HALF], tokens_in[:, HALF:]
            return (nt(a, lo) + nt(b, hi) if left else nt(lo, a) + nt(hi, b)).astype(BF)

        qbuf[...] = project(0, queries_in, True)
        kbuf[0:count, :] = project(1, keys_in, False)
        vbuf[:, 0:count] = project(2, keys_in, True)

        def two(p, _):
            keys = kbuf[0:count, pl.ds(pl.multiple_of(128 * p, 128), 128)]
            for j in range(2):
                at = rows16(128 * p + HDIM * j, HDIM)
                scores = jnp.dot(
                    keys[:, HDIM * j : HDIM * (j + 1)], qbuf[at, :], preferred_element_type=F32
                ) * (HDIM**-0.5)
                if mask is not None:
                    scores = jnp.where(mask, scores, -1e30)
                expo = jnp.exp(scores - jnp.max(scores, 0, keepdims=True))
                total = jnp.sum(expo, 0, keepdims=True)
                obuf[at, :] = (
                    jnp.dot(vbuf[at, 0:count], expo.astype(BF), preferred_element_type=F32) / total
                )
            if between:
                between(p)
            return 0

        lax.fori_loop(0, HEADS // 2, two, 0)

    siblings(0)
    attend(0, nbuf, nown, XL, None, lambda p: step(1, p + 1))
    sendb[...] = obuf[...].T.reshape(GX, 2, D).astype(BF)

    def k_copy(i):
        return rcopy(sendb.at[i], mixed.at[dep], k_s.at[i], k_r, i, 2 * inl + c)

    def k_start(i, _):
        here = jnp.logical_and(i == gx, me_too)

        @pl.when(jnp.logical_not(here))
        def _():
            k_copy(i).start()

        @pl.when(here)
        def _():
            pltpu.make_async_copy(sendb.at[i], mixed.at[dep], k_r).start()

        return 0

    lax.fori_loop(0, 64, k_start, 0)

    def depth_step(s, _):
        step(1, s)
        return 0

    lax.fori_loop(7, 11, depth_step, 0)

    own_c.wait()
    for d in range(1, 8):
        c_copy(d).wait_recv()
    which = which_axis((MINE, D))
    odd = lax.broadcasted_iota(jnp.int32, (MINE, D), 0) % 2
    first = XLD * gx + 2 * c
    cross = jnp.where(odd == 0, enc[pl.ds(first, 1), :], enc[pl.ds(first + 1, 1), :])
    pos = jnp.where(which == 1, cross, jnp.where(which == 0, enc[pl.ds(x, 1), :], dep2[...]))
    stream = jnp.transpose(cols[...].astype(F32), (0, 2, 1, 3)).reshape(MINE, D) + pos

    def project_out(v, base):
        return jnp.concatenate(
            [
                jnp.dot(v, w[k, base : base + D, :], preferred_element_type=F32)
                for k in range(2)
            ],
            1,
        )

    pltpu.make_async_copy(mixed, mixed, k_r).wait()
    stream = stream + project_out(mixed[...].reshape(MINE, D), QKV)
    nown[...] = normed(stream, gains[1:2, :])
    mask = (
        lax.broadcasted_iota(jnp.int32, (MINE, MINE), 0)
        + lax.broadcasted_iota(jnp.int32, (MINE, MINE), 1)
    ) % 2 == 0
    siblings(1)
    attend(SPAN, nown, nown, MINE, mask, None)
    stream = stream + project_out(obuf[...].T.astype(BF), SPAN + QKV)
    nown[...] = normed(stream, gains[2:3, :])

    def chip(d):
        return ((x + d) % XN) * 2 + c

    def to_near(d):
        n = 0 if d == 1 else 1
        return rcopy(nown, tokens.at[d, c], g_s.at[n], g_r.at[n], gx, chip(d))

    def to_far(n):
        rows = pl.ds(64 * n, 64)
        return rcopy(
            tokens.at[1 if n == 0 else 3, c, rows], tokens.at[2, c, rows],
            g_s.at[2 + n], g_r.at[2 + n], gx, chip(1 if n == 0 else 3),
        )

    def to_sib(d):
        src = nown if d == 0 else tokens.at[d, c]
        return rcopy(src, tokens.at[d, c], a_s.at[d], a_r.at[d], gx, sib)

    def from_sib(d):
        here = tokens.at[d, 1 - c]
        return rcopy(here, here, a_s.at[d], a_r.at[d], gx, sib)

    def pair_copy(d):
        return rcopy(sent.at[d, 1 - c], pair.at[d], q_s.at[d], q_r.at[d], gx, sib)

    def home(d):
        n = 0 if d == 1 else 1
        return rcopy(sums.at[d], got.at[d], s_s.at[n], s_r.at[n], gx, chip(4 - d))

    def home_far(n, hop):
        rows = pl.ds(64 * n, 64)
        src, dst = (sums.at[2, rows], stage.at[n]) if hop == 0 else (stage.at[n], got.at[2, rows])
        k = 2 + 2 * hop + n
        return rcopy(src, dst, s_s.at[k], s_r.at[k], gx, chip(1 if n == 0 else 3))

    to_near(1).start()
    to_near(3).start()
    to_sib(0).start()
    own_n = pltpu.make_async_copy(nown, tokens.at[0, c], l_s.at[10])
    own_n.start()
    loads[2].wait()
    loads[3].wait()

    def hidden_part(d):
        rows = tokens[d].reshape(2 * MINE, D)
        hidden = jax.nn.gelu(jnp.dot(rows, up[...], preferred_element_type=F32)).astype(BF)
        part = jnp.dot(hidden, down[...], preferred_element_type=F32).astype(BF)
        sent[d] = part.reshape(2, MINE, D)
        pair_copy(d).start()

    def both(d):
        pair_copy(d).wait_recv()
        return sent[d, c].astype(F32) + pair[d].astype(F32)

    own_n.wait()
    from_sib(0).wait_recv()
    hidden_part(0)
    for n, d in ((0, 1), (1, 3)):
        to_near(d).wait_recv()
        to_far(n).start()
        to_sib(d).start()
    from_sib(1).wait_recv()
    hidden_part(1)
    for n in range(2):
        to_far(n).wait_recv()
    to_sib(2).start()
    from_sib(3).wait_recv()
    hidden_part(3)
    sums[1] = both(1).astype(BF)
    home(1).start()
    from_sib(2).wait_recv()
    hidden_part(2)
    sums[3] = both(3).astype(BF)
    home(3).start()
    sums[2] = both(2).astype(BF)
    for n in range(2):
        home_far(n, 0).start()
    stream = stream + both(0)
    for n in range(2):
        home_far(n, 0).wait_recv()
        home_far(n, 1).start()
    for d in (1, 3):
        home(d).wait_recv()
        stream = stream + got[d].astype(F32)
    for n in range(2):
        home_far(n, 1).wait_recv()
    stream = stream + got[2].astype(F32)

    fbuf[...] = stream.astype(BF)

    def f_copy(d):
        there = (gz + d) % GZ
        return rcopy(fbuf.at[rows16(16 * there, 16)], frecv.at[gz], f_s.at[d - 1], f_r.at[d - 1], gx, there)

    own_f = pltpu.make_async_copy(fbuf.at[rows16(16 * gz, 16)], frecv.at[gz], l_s.at[11])
    own_f.start()
    for d in range(1, 8):
        f_copy(d).start()
    thick = jax.nn.softplus(jnp.sum(stream * head_w[...], -1, keepdims=True) + head_b[0, 0])
    i = lax.broadcasted_iota(jnp.int32, (MINE, MINE), 0)
    j = lax.broadcasted_iota(jnp.int32, (MINE, MINE), 1)
    across = jnp.broadcast_to(thick, (MINE, MINE)).T
    keep = jnp.logical_and(j <= i, (i + j) % 2 == 0)
    line = jnp.sum(jnp.where(keep, across, 0.0), 1, keepdims=True)
    gbuf[...] = jnp.broadcast_to(line, (MINE, 128))

    def h_copy(d):
        there = (gz + d) % GZ
        return rcopy(gbuf.at[rows16(16 * there, 16)], trecv.at[gz], h_s.at[d - 1], h_r.at[d - 1], gx, there)

    own_h = pltpu.make_async_copy(gbuf.at[rows16(16 * gz, 16)], trecv.at[gz], l_s.at[12])
    own_h.start()
    for d in range(1, 8):
        h_copy(d).start()
    own_f.wait()
    for d in range(1, 8):
        f_copy(d).wait_recv()
    feat[...] = (
        jnp.transpose(frecv[...].astype(F32).reshape(GZ, DPD, 2, D), (0, 2, 1, 3))
        .reshape(INL, XLD, DPD, D)
        .astype(BF)
    )
    own_h.wait()
    for d in range(1, 8):
        h_copy(d).wait_recv()
    row = lax.broadcasted_iota(jnp.int32, (GZ, 16, 128), 1)
    lane = lax.broadcasted_iota(jnp.int32, (GZ, 16, 128), 2)
    for k in range(2):
        mark = jnp.logical_and(row // 2 == lane, row % 2 == k)
        picked = jnp.sum(jnp.where(mark, trecv[...], 0.0), 1)
        for n in range(GZ):
            time[n // 2, 2 * (n % 2) + k : 2 * (n % 2) + k + 1, :] = picked[n : n + 1, :DPD]

    for d in range(1, 4):
        y_copy(d).wait_send()
    for d in range(1, 8):
        c_copy(d).wait_send()
        f_copy(d).wait_send()
        h_copy(d).wait_send()

    def t_end(i, _):
        @pl.when(jnp.logical_not(jnp.logical_and(32 * c + i == gx, own_line)))
        def _():
            t_copy(i).wait_send()

        return 0

    lax.fori_loop(0, 32, t_end, 0)

    def k_end(i, _):
        @pl.when(jnp.logical_not(jnp.logical_and(i == gx, me_too)))
        def _():
            k_copy(i).wait_send()

        return 0

    lax.fori_loop(0, 64, k_end, 0)
    l_copy().wait_send()
    for kind in range(2):
        for way in range(2):
            ring(kind, way, 1, True).wait_send()

        def r_end(s, _):
            ring(kind, 0, s).wait_send()

            @pl.when(s < 8)
            def _():
                ring(kind, 1, s).wait_send()

            return 0

        lax.fori_loop(2, 9, r_end, 0)

        def w_end(k, _):
            zsrc = (z + k) % ZN

            @pl.when(k > 0)
            def _():
                for cp in spread(kind, zsrc):
                    cp.wait_send()
                onward(kind, zsrc).wait_send()

            for cp in relay(kind, zsrc):
                cp.wait_send()
            return 0

        lax.fori_loop(0, ZN, w_end, 0)
    for d in (1, 3):
        to_near(d).wait_send()
        home(d).wait_send()
    for n in range(2):
        to_far(n).wait_send()
        home_far(n, 0).wait_send()
        home_far(n, 1).wait_send()
    for d in range(4):
        to_sib(d).wait_send()
        pair_copy(d).wait_send()


def body(
    tokens, cross_qkv, cross_out, depth_qkv, depth_out, up_proj, down_proj, gains, head_weight, head_bias
):
    enc = table()
    dep2 = jnp.asarray(np.repeat(enc[:DP], 2, 0))
    enc = jnp.asarray(enc)
    dma = pltpu.SemaphoreType.DMA
    vmem = pltpu.VMEM
    return pl.pallas_call(
        block_kernel,
        out_shape=(
            jax.ShapeDtypeStruct((INL, XLD, DPD, D), BF),
            jax.ShapeDtypeStruct((INL, XLD, DPD), F32),
        ),
        in_specs=[VM] * 7 + [pl.BlockSpec(memory_space=pltpu.SMEM), VM] + [ANY] * 4,
        out_specs=(VM, VM),
        scratch_shapes=[
            vmem((XL, D), F32),
            vmem((MINE, D), F32),
            vmem((D, FF // GZ), BF),
            vmem((FF // GZ, D), BF),
            vmem((SLOT, D), F32),
            vmem((2, SLOT, HALF), BF),
            vmem((YN, SLOT, HALF), BF),
            vmem((BLOCK, HALF), BF),
            vmem((2, 2 * SPAN, HALF), BF),
            vmem((LINES, XLD, D), BF),
            vmem((GX, XLD, D), BF),
            vmem((GZ, 2, DPD, D), BF),
            vmem((XL, D), BF),
            vmem((XL, D), BF),
            vmem((D, MINE), BF),
            vmem((D, XL), BF),
            vmem((D, MINE), F32),
            vmem((GX, 2, D), BF),
            vmem((DP, 2, D), BF),
            vmem((MINE, D), BF),
            vmem((4, 2, MINE, D), BF),
            vmem((4, 2, MINE, D), BF),
            vmem((4, MINE, D), BF),
            vmem((4, MINE, D), BF),
            vmem((4, MINE, D), BF),
            vmem((2, 64, D), BF),
            vmem((MINE, D), BF),
            vmem((MINE, 128), F32),
            vmem((GZ, 16, D), BF),
            vmem((GZ, 16, 128), F32),
            dma((3,)), dma((3,)),
            dma((32,)), dma,
            dma((7,)), dma((7,)),
            dma((2, 2, 8)), dma((2, 2, 8)),
            dma((2, ZN, 3)), dma((2, ZN, 3)),
            dma((2, ZN, 2)), dma((2, ZN, 2)),
            dma, dma,
            dma((64,)), dma,
            dma((4,)), dma((4,)),
            dma((4,)), dma((4,)),
            dma((4,)), dma((4,)),
            dma((6,)), dma((6,)),
            dma((7,)), dma((7,)),
            dma((7,)), dma((7,)),
            dma((13,)),
        ],
        compiler_params=pltpu.CompilerParams(
            collective_id=0, has_side_effects=True, vmem_limit_bytes=LIMIT
        ),
        name="axial_block",
    )(
        tokens, cross_qkv, cross_out, depth_qkv, depth_out, gains, head_weight[None], head_bias[None],
        jnp.asarray(packing(), BF), enc, dep2, up_proj, down_proj,
    )


def solution(mesh):
    return jax.shard_map(
        body,
        mesh=mesh,
        in_specs=(
            P(None, "gx", "gz", None),
            P(None, "gx"),
            P("gx", None),
            P(None, "gx"),
            P("gx", None),
            P(None, "gz"),
            P("gz", None),
            P(),
            P(),
            P(),
        ),
        out_specs=(P(None, "gx", "gz", None), P(None, "gx", "gz")),
        check_vma=False,
    )
```

time: 773 us -> 150 us (0.19)
  waiting for transfers between devices: 649 us -> 0 us
  Pallas kernels: 0 us -> 143 us
  local copies, waits for them, and re-layouts: 41.9 us -> 5.97 us
  matrix products: 24.7 us -> 0 us
  starting transfers between devices: 23.1 us -> 0 us
  between operations: 15.2 us -> 1.3 us
  blocking collectives: 13.5 us -> 0 us
    all_gather x7 -> x0, waiting for transfers between devices: 563 us -> none  [the longest x1 143 us: body(): lax.all_gather(depth_qkv, 'gx', axis=1, tiled=True)]
    pallas_call x0 -> x1, Pallas kernels: none -> 143 us  [body(): pl.pallas_call(block_kernel, out_shape=(jax.ShapeDtypeStruct((INL, XLD, D...]
    all_to_all x4 -> x0, waiting for transfers between devices: 45.6 us -> none  [the longest x1 15.4 us: body(): lax.all_to_all(lined[1], 'gx', split_axis=0, concat_axis=2, tiled=True)]
    reduce_scatter x1 -> x0, waiting for transfers between devices: 37.5 us -> none  [body(): lax.psum_scatter(jnp.dot(hidden, down_proj, preferred_element_type=jnp.fl...]
    all_to_all x4 -> x0, starting transfers between devices: 22.6 us -> none  [the longest x1 8.72 us: body(): lax.all_to_all(lined[1], 'gx', split_axis=0, concat_axis=2, tiled=True)]
    unnamed x27 -> x8, local copies, waits for them, and re-layouts: 23.7 us -> 4.71 us
    dot_general x8 -> x0, matrix products: 18.2 us -> none  [the longest x2 4.8 us: attend(): jnp.einsum('...qk,...ke->...qe', weights, values, preferred_element_type=...]
    all_gather x1 -> x0, blocking collectives: 13.5 us -> none  [carried_in(): everything = lax.all_gather(shard, axis)]
  transfers between devices with their start and end apart: 12 -> 0, of which waited for: 11 -> 0; matrix products, arithmetic and copies ran while one was open for 7% -> 0% of each run, Pallas kernels for 0% -> 0%
where the time goes in v2:
time: 150 us
  Pallas kernels  143 us (95%)
  local copies, waits for them, and re-layouts  5.97 us (4%)
    pallas_call x1, Pallas kernels, body(): pl.pallas_call(block_kernel, out_shape=(jax.ShapeDtypeStruct((INL, XLD, D...  143 us
    unnamed x8, local copies, waits for them, and re-layouts  4.71 us

profile of v2, /device:TPU:1, one launch (start us, length us, event | category | flops | bytes accessed | tf_op | source)
XLA Modules:
  0.0 150.2 jit_solution(12152682827689242253)
XLA Ops:
  1.3 1.3 broadcast_in_dim.6.head_w
  2.5 0.0 copy-start
  2.5 1.7 %copy.15.w1 = bf16[768,36]{1,0:T(8,128)(2,1)} copy(bf16[768,36]{0,1:T(8,128)(2,1)} %param.14) | data formatting | bytes 110592 | tf_op args[1]
  4.2 0.0 copy-done
  4.2 0.8 copy.16.w3
  5.0 143.0 %axial_block.1 = (bf16[4,4,8,768]{3,2,1,0:T(8,128)(2,1)}, f32[4,4,8]{2,1,0:T(4,128)}) custom-call(bf16[4,4,8,768]{3,2,1,0:T(8,128)(2,1)} %tok.1, bf16[768,36]{1,0:T(8,128)(2,1)} %copy.15.w1, bf16[12,768]{1,0:T(8,128)(2,1)} %w2.1, bf16[768,36]{1,0:T(8,128)(2,1)} %copy.16.w3, bf16[12,768]{1,0:T(8,128)(2,1)} %w4.1, f32[3,768]{1,0:T(4,128)} %gains.1, ...), custom_call_target="tpu_custom_call" | custom-call | tf_op jit(solution)/shard_map/axial_block/pallas_call | solution.py:660
  148.0 0.0 copy-start.1
  148.0 1.6 %copy.20 = bf16[4,4,8,768]{3,2,1,0:T(8,128)(2,1)} copy(bf16[4,4,8,768]{3,2,1,0:T(8,128)(2,1)} %get-tuple-element.4) | data formatting | bytes 393216
  149.6 0.0 copy-done.1
  149.6 0.6 copy.21
Async XLA Ops:
  2.5 1.7 %copy-start = (bf16[768,36]{0,1:T(8,128)(2,1)S(1)}, bf16[768,36]{0,1:T(8,128)(2,1)}, u32[]{:S(2)}) copy-start(bf16[768,36]{0,1:T(8,128)(2,1)} %param.16) | copy-start | bytes 165892
  148.0 1.6 %copy-start.1 = (f32[4,4,8]{2,1,0:T(4,128)S(1)}, f32[4,4,8]{2,1,0:T(4,128)}, u32[]{:S(2)}) copy-start(f32[4,4,8]{2,1,0:T(4,128)} %get-tuple-element.5) | copy-start | bytes 1540

commit v3 on v2

--- a/solution.py
+++ b/solution.py
@@ -21,8 +21,8 @@
 KIND = QKV_ROWS + OUT_ROWS
 BLOCK = 2 * KIND
 QKV, SPAN = 3 * D, 4 * D
-PIECE = 48
-SLOT = 112
+PIECE, SUB = 48, 16
+SLOT = 48
 MESH = pl.DeviceIdType.MESH
 BF, F32 = jnp.bfloat16, jnp.float32
 ANY = pl.BlockSpec(memory_space=pl.ANY)
@@ -38,9 +38,9 @@
 
 
 def packing():
-    one = np.zeros((BLOCK, YN * SLOT), np.float32)
+    one = np.zeros((KIND, YN * SLOT), np.float32)
     row = 0
-    for at, count in ((0, 36), (40, 12), (56, 36), (96, 12)):
+    for at, count in ((0, 36), (36, 12)):
         for y in range(YN):
             for r in range(count):
                 one[row, y * SLOT + at + r] = 1
@@ -85,10 +85,10 @@
 def block_kernel(
     tok, w1, w2, w3, w4, gains, head_w, head_b, one_ref, enc_h, dep2_h, up_h, down_h,
     feat, time,
-    enc, dep2, up, down, sbuf, shard, ybuf, block, w, by_line, lines, cols, nbuf,
-    kbuf, qbuf, vbuf, obuf, sendb, mixed, nown, tokens, sent, pair, sums, got, stage, fbuf, gbuf, frecv, trecv,
-    y_s, y_r, t_s, t_r, c_s, c_r, z_s, z_r, p_s, p_r, b_s, b_r, i_s, i_r, k_s, k_r,
-    g_s, g_r, a_s, a_r, q_s, q_r, s_s, s_r, f_s, f_r, h_s, h_r, l_s,
+    enc, dep2, up, down, sbuf, shard, mine_y, ybuf, block, w, by_line, lines, cols, nbuf,
+    kbuf, qbuf, vbuf, obuf, sendb, mixed, nown, pairtok, acc, sent, pair, fbuf, gbuf, frecv, trecv,
+    y_s, y_r, t_s, t_r, c_s, c_r, z_s, z_r, x_s, x_r, p_s, p_r, b_s, b_r, i_s, i_r, k_s, k_r,
+    m_s, m_r, a_s, a_r, f_s, f_r, h_s, h_r, l_s,
 ):
     gx, gz, z, y, x, c = place()
     half = gx // 32
@@ -121,41 +121,40 @@
     lax.fori_loop(0, 64, greet_back, 0)
     for d in range(1, 4):
         signal(z * YN + (y + d) % YN, gz)
-    signal(((z + 1) % ZN) * YN + y, gz)
-    signal(((z + 15) % ZN) * YN + y, gz)
+    for d in range(1, ZN):
+        signal(((z + d) % ZN) * YN + y, gz)
     for d in range(1, 8):
         signal(gx, (gz + d) % GZ)
 
     loads = [
         pltpu.make_async_copy(a, b, l_s.at[k])
-        for k, (a, b) in enumerate(((enc_h, enc), (dep2_h, dep2), (up_h, up), (down_h, down)))
+        for k, (a, b) in enumerate(((enc_h, enc), (dep2_h, dep2), (up_h, up.at[x]), (down_h, down.at[x])))
     ]
     for load in loads:
         load.start()
-    sbuf[...] = jnp.zeros_like(sbuf)
-    sbuf[0:36, :] = w1[...].astype(F32).T
-    sbuf[40:52, :] = w2[...].astype(F32)
-    sbuf[56:92, :] = w3[...].astype(F32).T
-    sbuf[96:108, :] = w4[...].astype(F32)
-    shard[0] = sbuf[:, :HALF].astype(BF)
-    shard[1] = sbuf[:, HALF:].astype(BF)
+    for kind, (a, b) in enumerate(((w1, w2), (w3, w4))):
+        sbuf[0:36, :] = a[...].astype(F32)
+        sbuf[36:48, :] = b[...].astype(F32)
+        shard[0, kind] = sbuf[:, :HALF].astype(BF)
+        shard[1, kind] = sbuf[:, HALF:].astype(BF)
     by_line[...] = (
         jnp.transpose(tok[...].astype(F32), (0, 2, 1, 3)).reshape(LINES, XLD, D).astype(BF)
     )
     pl.semaphore_wait(
         pltpu.get_barrier_semaphore(),
-        12 + 32 + 64 - jnp.where(own_line, 1, 0) - jnp.where(me_too, 1, 0),
+        25 + 32 + 64 - jnp.where(own_line, 1, 0) - jnp.where(me_too, 1, 0),
     )
 
-    def y_copy(d):
+    def y_copy(kind, d):
         return rcopy(
-            shard.at[c], ybuf.at[y], y_s.at[d - 1], y_r.at[d - 1], z * YN + (y + d) % YN, gz
-        )
-
-    own_y = pltpu.make_async_copy(shard.at[c], ybuf.at[y], l_s.at[4])
+            shard.at[c, kind], ybuf.at[kind, y], y_s.at[kind, d - 1], y_r.at[kind, d - 1],
+            z * YN + (y + d) % YN, gz,
+        )
+
+    own_y = pltpu.make_async_copy(shard.at[c], mine_y, l_s.at[4])
     own_y.start()
     for d in (1, 3, 2):
-        y_copy(d).start()
+        y_copy(0, d).start()
 
     def t_copy(i):
         return rcopy(by_line.at[i], lines.at[gx], t_s.at[i], t_r, 32 * c + i, 2 * x + half)
@@ -186,20 +185,40 @@
     for d in range(1, 8):
         c_copy(d).start()
 
+    for d in (1, 3, 2):
+        y_copy(1, d).start()
     own_y.wait()
-    for d in range(1, 4):
-        y_copy(d).wait_recv()
-    block[...] = jnp.dot(
-        one_ref[...], ybuf[...].reshape(YN * SLOT, HALF), preferred_element_type=F32
-    ).astype(BF)
-
-    def who(kind):
-        return x if kind else y
-
-    def near(kind, d):
-        if kind:
-            return gx, ((x + d) % XN) * 2 + c
-        return z * YN + (y + d) % YN, gz
+
+    def pack(kind):
+        for d in range(1, 4):
+            y_copy(kind, d).wait_recv()
+        for k in range(YN):
+
+            @pl.when(k == y)
+            def _():
+                ybuf[kind, k] = mine_y[kind]
+
+        block[KIND * kind : KIND * (kind + 1), :] = jnp.dot(
+            one_ref[...], ybuf[kind].reshape(YN * SLOT, HALF), preferred_element_type=F32
+        ).astype(BF)
+
+    pack(0)
+
+    def who(zsrc):
+        return jnp.where(zsrc % 2 == 0, y, x)
+
+    def seat(zsrc):
+        return jnp.where(zsrc % 2 == 0, x, y)
+
+    def near_x(d):
+        return gx, ((x + d) % XN) * 2 + c
+
+    def near(zsrc, d):
+        even = zsrc % 2 == 0
+        return (
+            jnp.where(even, z * YN + (y + d) % YN, gx),
+            jnp.where(even, gz, ((x + d) % XN) * 2 + c),
+        )
 
     def piece(kind, zsrc, k):
         at = SPAN * kind + jnp.where(k < 3, QKV_ROWS * zsrc + PIECE * k, QKV + PIECE * zsrc)
@@ -220,37 +239,36 @@
         for kind in range(2)
         for k in range(2)
     ]
-    for cp in own_parts:
-        cp.start()
-
-    def ring(kind, way, s, first=False):
-        back = s - 1
-        zsrc = (z + (ZN - back if way == 0 else back)) % ZN
-        znext = (z + (1 if way == 0 else ZN - 1)) % ZN
-        to = piece(kind, zsrc, who(kind))
-        src = block.at[rows16(KIND * kind + PIECE * who(kind), PIECE)] if first else to
+    def sub(kind, zsrc, n):
+        at = QKV_ROWS * zsrc + PIECE * who(zsrc) + SUB * n
+        out = QKV + PIECE * zsrc + SUB * n
+        return w.at[c, rows16(SPAN * kind + jnp.where(who(zsrc) < 3, at, out), SUB)]
+
+    def z_copy(kind, d):
+        at = KIND * kind + PIECE * who(z) + SUB * seat(z)
         return rcopy(
-            src, to, z_s.at[kind, way, s - 1], z_r.at[kind, way, s - 1], znext * YN + y, gz
-        )
-
-    def arrived(kind, way, s):
-        zsrc = (z + (ZN - s if way == 0 else s)) % ZN
-        here = piece(kind, zsrc, who(kind))
-        rcopy(here, here, z_s.at[kind, way, s - 1], z_r.at[kind, way, s - 1], gx, gz).wait_recv()
-        return zsrc
+            block.at[rows16(at, SUB)], sub(kind, z, seat(z)),
+            z_s.at[kind, d - 1], z_r.at[kind, d - 1], ((z + d) % ZN) * YN + y, gz,
+        )
+
+    def x_copy(kind, zsrc, d):
+        mine = sub(kind, zsrc, seat(zsrc))
+        return rcopy(
+            mine, mine, x_s.at[kind, zsrc, d - 1], x_r.at[kind, zsrc, d - 1], *near(zsrc + 1, d)
+        )
 
     def spread(kind, zsrc):
-        mine = piece(kind, zsrc, who(kind))
+        mine = piece(kind, zsrc, who(zsrc))
         return [
-            rcopy(mine, mine, p_s.at[kind, zsrc, n], p_r.at[kind, zsrc, n], *near(kind, d))
+            rcopy(mine, mine, p_s.at[kind, zsrc, n], p_r.at[kind, zsrc, n], *near(zsrc, d))
             for n, d in enumerate((1, 3))
         ]
 
     def onward(kind, zsrc):
-        odd = zsrc % 2
-        it = piece(kind, zsrc, (who(kind) + jnp.where(odd == 0, 3, 1)) % 4)
+        turn = (zsrc // 2) % 2
+        it = piece(kind, zsrc, (who(zsrc) + jnp.where(turn == 0, 3, 1)) % 4)
         return rcopy(
-            it, it, p_s.at[kind, zsrc, 2], p_r.at[kind, zsrc, 2], *near(kind, jnp.where(odd == 0, 1, 3))
+            it, it, p_s.at[kind, zsrc, 2], p_r.at[kind, zsrc, 2], *near(zsrc, jnp.where(turn == 0, 1, 3))
         )
 
     def relay(kind, zsrc):
@@ -261,62 +279,68 @@
 
     def collect_near(kind, zsrc):
         for n, d in enumerate((3, 1)):
-            here = piece(kind, zsrc, (who(kind) + d) % 4)
+            here = piece(kind, zsrc, (who(zsrc) + d) % 4)
             rcopy(here, here, p_s.at[kind, zsrc, n], p_r.at[kind, zsrc, n], gx, gz).wait_recv()
         onward(kind, zsrc).start()
 
     def collect_far(kind, zsrc):
-        here = piece(kind, zsrc, (who(kind) + 2) % 4)
+        here = piece(kind, zsrc, (who(zsrc) + 2) % 4)
         rcopy(here, here, p_s.at[kind, zsrc, 2], p_r.at[kind, zsrc, 2], gx, gz).wait_recv()
         for cp in relay(kind, zsrc):
             cp.start()
 
     def begin(kind):
-        for way in range(2):
-            ring(kind, way, 1, True).start()
+        for cp in own_parts[2 * kind : 2 * kind + 2]:
+            cp.start()
+
+        @pl.when(seat(z) < 3)
+        def _():
+            for k in range(1, 9):
+                z_copy(kind, k).start()
+                if k < 8:
+                    z_copy(kind, ZN - k).start()
+
         for cp in own_parts[2 * kind : 2 * kind + 2]:
             cp.wait()
         for cp in relay(kind, z):
             cp.start()
 
-    def step(kind, s):
-        @pl.when(s <= 8)
-        def _():
-            zsrc = arrived(kind, 0, s)
-
-            @pl.when(s < 8)
+    def source(i):
+        d = jnp.where(i % 2 == 0, i // 2 + 1, ZN - 1 - i // 2)
+        return (z + ZN - d) % ZN, d
+
+    def stage(lag, i, do):
+        @pl.when(jnp.logical_and(i >= lag, i < ZN - 1 + lag))
+        def _():
+            do(*source(i - lag))
+
+    def step(kind, i):
+        def from_z(zsrc, d):
+            @pl.when(seat(zsrc) < 3)
             def _():
-                ring(kind, 0, s + 1).start()
+                here = sub(kind, zsrc, seat(zsrc))
+                rcopy(here, here, z_s.at[kind, d - 1], z_r.at[kind, d - 1], gx, gz).wait_recv()
+                for k in (1, 3, 2):
+                    x_copy(kind, zsrc, k).start()
+
+        def whole(zsrc, _):
+            for k in range(1, 4):
+                n = (seat(zsrc) + 4 - k) % 4
+
+                @pl.when(n < 3)
+                def _():
+                    here = sub(kind, zsrc, n)
+                    rcopy(
+                        here, here, x_s.at[kind, zsrc, k - 1], x_r.at[kind, zsrc, k - 1], gx, gz
+                    ).wait_recv()
 
             for cp in spread(kind, zsrc):
                 cp.start()
 
-        @pl.when(s <= 7)
-        def _():
-            zsrc = arrived(kind, 1, s)
-
-            @pl.when(s < 7)
-            def _():
-                ring(kind, 1, s + 1).start()
-
-            for cp in spread(kind, zsrc):
-                cp.start()
-
-        @pl.when(jnp.logical_and(s >= 2, s <= 9))
-        def _():
-            collect_near(kind, (z + ZN - s + 1) % ZN)
-
-        @pl.when(jnp.logical_and(s >= 2, s <= 8))
-        def _():
-            collect_near(kind, (z + s - 1) % ZN)
-
-        @pl.when(jnp.logical_and(s >= 3, s <= 10))
-        def _():
-            collect_far(kind, (z + ZN - s + 2) % ZN)
-
-        @pl.when(jnp.logical_and(s >= 3, s <= 9))
-        def _():
-            collect_far(kind, (z + s - 2) % ZN)
+        stage(0, i, from_z)
+        stage(3, i, whole)
+        stage(6, i, lambda zsrc, _: collect_near(kind, zsrc))
+        stage(9, i, lambda zsrc, _: collect_far(kind, zsrc))
 
     def siblings(kind):
         def one(zsrc, _):
@@ -332,20 +356,85 @@
 
     begin(0)
 
-    def cross_step(s, _):
-        step(0, s)
-
-        @pl.when(s == 6)
+    def ring4(near_of, me, own, item, part, at):
+        def first(n):
+            return rcopy(own, item(me), m_s.at[at, n], m_r.at[at, n], *near_of((1, 3)[n]))
+
+        def second(n):
+            src = part((me + (3, 1)[n]) % 4, n)
+            return rcopy(src, src, m_s.at[at, 2 + n], m_r.at[at, 2 + n], *near_of((1, 3)[n]))
+
+        return first, second
+
+    def near_y(d):
+        return z * YN + (y + d) % YN, gz
+
+    up_rings = [
+        ring4(
+            near_x, x, up_h.at[pl.ds(HALF * k, HALF)],
+            lambda chip, k=k: up.at[chip, pl.ds(HALF * k, HALF)],
+            lambda chip, n, k=k: up.at[chip, pl.ds(HALF * k + HALF // 2 * n, HALF // 2)],
+            k,
+        )
+        for k in range(2)
+    ]
+
+    def quarter(chip, n=None, q=None):
+        at = 96 * (y if q is None else q)
+        return down.at[chip, rows16(at, 96) if n is None else rows16(at + 48 * n, 48)]
+
+    down_ring = ring4(near_x, x, down_h.at[rows16(96 * y, 96)], quarter, quarter, 2)
+    down_spread = []
+    for d in (1, 3, 2):
+        chip = (x + d) % XN
+        down_spread.append(
+            ring4(
+                near_y, y, quarter(chip),
+                lambda q, chip=chip: quarter(chip, None, q),
+                lambda q, n, chip=chip: quarter(chip, n, q),
+                2 + d,
+            )
+        )
+    all_rings = [*up_rings, down_ring, *down_spread]
+
+    def firsts(r):
+        for n in range(2):
+            r[0](n).start()
+
+    def seconds(r):
+        for n in range(2):
+            r[0](n).wait_recv()
+        for n in range(2):
+            r[1](n).start()
+
+    def finished(r):
+        for n in range(2):
+            r[1](n).wait_recv()
+
+    firsts(down_ring)
+    firsts(up_rings[0])
+
+    def cross_step(i, _):
+        step(0, i)
+
+        @pl.when(i == 8)
+        def _():
+            pack(1)
+            begin(1)
+
+        @pl.when(i == 10)
         def _():
             mine = lines.at[rows16(32 * c, 32)]
             pltpu.make_async_copy(mine, mine, t_r).wait()
             l_copy().start()
 
+        @pl.when(i >= 18)
+        def _():
+            step(1, i - 18)
+
         return 0
 
-    lax.fori_loop(1, 9, cross_step, 0)
-    begin(1)
-    lax.fori_loop(9, 11, cross_step, 0)
+    lax.fori_loop(0, 24, cross_step, 0)
 
     loads[0].wait()
     loads[1].wait()
@@ -392,7 +481,12 @@
         lax.fori_loop(0, HEADS // 2, two, 0)
 
     siblings(0)
-    attend(0, nbuf, nown, XL, None, lambda p: step(1, p + 1))
+
+    def depth_step(i, _):
+        step(1, i)
+        return 0
+
+    attend(0, nbuf, nown, XL, None, lambda p: depth_step(6 + p, 0))
     sendb[...] = obuf[...].T.reshape(GX, 2, D).astype(BF)
 
     def k_copy(i):
@@ -413,11 +507,12 @@
 
     lax.fori_loop(0, 64, k_start, 0)
 
-    def depth_step(s, _):
-        step(1, s)
-        return 0
-
-    lax.fori_loop(7, 11, depth_step, 0)
+    lax.fori_loop(12, 24, depth_step, 0)
+    firsts(up_rings[1])
+    seconds(down_ring)
+    seconds(up_rings[0])
+    firsts(down_spread[0])
+    firsts(down_spread[1])
 
     own_c.wait()
     for d in range(1, 8):
@@ -445,98 +540,43 @@
         lax.broadcasted_iota(jnp.int32, (MINE, MINE), 0)
         + lax.broadcasted_iota(jnp.int32, (MINE, MINE), 1)
     ) % 2 == 0
+    finished(down_ring)
+    firsts(down_spread[2])
     siblings(1)
+    seconds(down_spread[0])
+    seconds(down_spread[1])
+    seconds(up_rings[1])
     attend(SPAN, nown, nown, MINE, mask, None)
     stream = stream + project_out(obuf[...].T.astype(BF), SPAN + QKV)
     nown[...] = normed(stream, gains[2:3, :])
 
-    def chip(d):
-        return ((x + d) % XN) * 2 + c
-
-    def to_near(d):
-        n = 0 if d == 1 else 1
-        return rcopy(nown, tokens.at[d, c], g_s.at[n], g_r.at[n], gx, chip(d))
-
-    def to_far(n):
-        rows = pl.ds(64 * n, 64)
-        return rcopy(
-            tokens.at[1 if n == 0 else 3, c, rows], tokens.at[2, c, rows],
-            g_s.at[2 + n], g_r.at[2 + n], gx, chip(1 if n == 0 else 3),
-        )
-
-    def to_sib(d):
-        src = nown if d == 0 else tokens.at[d, c]
-        return rcopy(src, tokens.at[d, c], a_s.at[d], a_r.at[d], gx, sib)
-
-    def from_sib(d):
-        here = tokens.at[d, 1 - c]
-        return rcopy(here, here, a_s.at[d], a_r.at[d], gx, sib)
-
-    def pair_copy(d):
-        return rcopy(sent.at[d, 1 - c], pair.at[d], q_s.at[d], q_r.at[d], gx, sib)
-
-    def home(d):
-        n = 0 if d == 1 else 1
-        return rcopy(sums.at[d], got.at[d], s_s.at[n], s_r.at[n], gx, chip(4 - d))
-
-    def home_far(n, hop):
-        rows = pl.ds(64 * n, 64)
-        src, dst = (sums.at[2, rows], stage.at[n]) if hop == 0 else (stage.at[n], got.at[2, rows])
-        k = 2 + 2 * hop + n
-        return rcopy(src, dst, s_s.at[k], s_r.at[k], gx, chip(1 if n == 0 else 3))
-
-    to_near(1).start()
-    to_near(3).start()
-    to_sib(0).start()
-    own_n = pltpu.make_async_copy(nown, tokens.at[0, c], l_s.at[10])
-    own_n.start()
+    def tok_copy():
+        return rcopy(nown, pairtok.at[c], a_s.at[0], a_r.at[0], gx, sib)
+
+    def sum_copy():
+        return rcopy(sent, pair, a_s.at[1], a_r.at[1], gx, sib)
+
+    seconds(down_spread[2])
+    tok_copy().start()
+    pairtok[c] = nown[...]
     loads[2].wait()
     loads[3].wait()
-
-    def hidden_part(d):
-        rows = tokens[d].reshape(2 * MINE, D)
-        hidden = jax.nn.gelu(jnp.dot(rows, up[...], preferred_element_type=F32)).astype(BF)
-        part = jnp.dot(hidden, down[...], preferred_element_type=F32).astype(BF)
-        sent[d] = part.reshape(2, MINE, D)
-        pair_copy(d).start()
-
-    def both(d):
-        pair_copy(d).wait_recv()
-        return sent[d, c].astype(F32) + pair[d].astype(F32)
-
-    own_n.wait()
-    from_sib(0).wait_recv()
-    hidden_part(0)
-    for n, d in ((0, 1), (1, 3)):
-        to_near(d).wait_recv()
-        to_far(n).start()
-        to_sib(d).start()
-    from_sib(1).wait_recv()
-    hidden_part(1)
-    for n in range(2):
-        to_far(n).wait_recv()
-    to_sib(2).start()
-    from_sib(3).wait_recv()
-    hidden_part(3)
-    sums[1] = both(1).astype(BF)
-    home(1).start()
-    from_sib(2).wait_recv()
-    hidden_part(2)
-    sums[3] = both(3).astype(BF)
-    home(3).start()
-    sums[2] = both(2).astype(BF)
-    for n in range(2):
-        home_far(n, 0).start()
-    stream = stream + both(0)
-    for n in range(2):
-        home_far(n, 0).wait_recv()
-        home_far(n, 1).start()
-    for d in (1, 3):
-        home(d).wait_recv()
-        stream = stream + got[d].astype(F32)
-    for n in range(2):
-        home_far(n, 1).wait_recv()
-    stream = stream + got[2].astype(F32)
+    there = pairtok.at[1 - c]
+    rcopy(there, there, a_s.at[0], a_r.at[0], gx, gz).wait_recv()
+
+    def hidden_part(k):
+        both = pairtok[...].reshape(2 * MINE, D)
+        hidden = jax.nn.gelu(jnp.dot(both, up[k], preferred_element_type=F32)).astype(BF)
+        return jnp.dot(hidden, down[k], preferred_element_type=F32)
+
+    for r in (*up_rings, *down_spread):
+        finished(r)
+    acc[...] = hidden_part(0) + hidden_part(1) + hidden_part(2) + hidden_part(3)
+    sent[...] = acc[pl.ds(pl.multiple_of(MINE * (1 - c), MINE), MINE), :].astype(BF)
+    sum_copy().start()
+    stream = stream + acc[pl.ds(pl.multiple_of(MINE * c, MINE), MINE), :]
+    sum_copy().wait_recv()
+    stream = stream + pair[...].astype(F32)
 
     fbuf[...] = stream.astype(BF)
 
@@ -548,7 +588,7 @@
     own_f.start()
     for d in range(1, 8):
         f_copy(d).start()
-    thick = jax.nn.softplus(jnp.sum(stream * head_w[...], -1, keepdims=True) + head_b[0, 0])
+    thick = jax.nn.softplus(jnp.sum(stream * head_w[...].reshape(1, D), -1, keepdims=True) + head_b[0])
     i = lax.broadcasted_iota(jnp.int32, (MINE, MINE), 0)
     j = lax.broadcasted_iota(jnp.int32, (MINE, MINE), 1)
     across = jnp.broadcast_to(thick, (MINE, MINE)).T
@@ -584,7 +624,8 @@
             time[n // 2, 2 * (n % 2) + k : 2 * (n % 2) + k + 1, :] = picked[n : n + 1, :DPD]
 
     for d in range(1, 4):
-        y_copy(d).wait_send()
+        y_copy(0, d).wait_send()
+        y_copy(1, d).wait_send()
     for d in range(1, 8):
         c_copy(d).wait_send()
         f_copy(d).wait_send()
@@ -609,25 +650,21 @@
     lax.fori_loop(0, 64, k_end, 0)
     l_copy().wait_send()
     for kind in range(2):
-        for way in range(2):
-            ring(kind, way, 1, True).wait_send()
-
-        def r_end(s, _):
-            ring(kind, 0, s).wait_send()
-
-            @pl.when(s < 8)
-            def _():
-                ring(kind, 1, s).wait_send()
-
-            return 0
-
-        lax.fori_loop(2, 9, r_end, 0)
+        @pl.when(seat(z) < 3)
+        def _():
+            for d in range(1, ZN):
+                z_copy(kind, d).wait_send()
 
         def w_end(k, _):
             zsrc = (z + k) % ZN
 
             @pl.when(k > 0)
             def _():
+                @pl.when(seat(zsrc) < 3)
+                def _():
+                    for d in range(1, 4):
+                        x_copy(kind, zsrc, d).wait_send()
+
                 for cp in spread(kind, zsrc):
                     cp.wait_send()
                 onward(kind, zsrc).wait_send()
@@ -637,16 +674,12 @@
             return 0
 
         lax.fori_loop(0, ZN, w_end, 0)
-    for d in (1, 3):
-        to_near(d).wait_send()
-        home(d).wait_send()
-    for n in range(2):
-        to_far(n).wait_send()
-        home_far(n, 0).wait_send()
-        home_far(n, 1).wait_send()
-    for d in range(4):
-        to_sib(d).wait_send()
-        pair_copy(d).wait_send()
+    for r in all_rings:
+        for n in range(2):
+            r[0](n).wait_send()
+            r[1](n).wait_send()
+    tok_copy().wait_send()
+    sum_copy().wait_send()
 
 
 def body(
@@ -668,11 +701,12 @@
         scratch_shapes=[
             vmem((XL, D), F32),
             vmem((MINE, D), F32),
-            vmem((D, FF // GZ), BF),
-            vmem((FF // GZ, D), BF),
+            vmem((XN, D, FF // GZ), BF),
+            vmem((XN, FF // GZ, D), BF),
             vmem((SLOT, D), F32),
+            vmem((2, 2, SLOT, HALF), BF),
             vmem((2, SLOT, HALF), BF),
-            vmem((YN, SLOT, HALF), BF),
+            vmem((2, YN, SLOT, HALF), BF),
             vmem((BLOCK, HALF), BF),
             vmem((2, 2 * SPAN, HALF), BF),
             vmem((LINES, XLD, D), BF),
@@ -686,28 +720,25 @@
             vmem((GX, 2, D), BF),
             vmem((DP, 2, D), BF),
             vmem((MINE, D), BF),
-            vmem((4, 2, MINE, D), BF),
-            vmem((4, 2, MINE, D), BF),
-            vmem((4, MINE, D), BF),
-            vmem((4, MINE, D), BF),
-            vmem((4, MINE, D), BF),
-            vmem((2, 64, D), BF),
+            vmem((2, MINE, D), BF),
+            vmem((2 * MINE, D), F32),
+            vmem((MINE, D), BF),
+            vmem((MINE, D), BF),
             vmem((MINE, D), BF),
             vmem((MINE, 128), F32),
             vmem((GZ, 16, D), BF),
             vmem((GZ, 16, 128), F32),
-            dma((3,)), dma((3,)),
+            dma((2, 3)), dma((2, 3)),
             dma((32,)), dma,
             dma((7,)), dma((7,)),
-            dma((2, 2, 8)), dma((2, 2, 8)),
+            dma((2, 15)), dma((2, 15)),
+            dma((2, ZN, 3)), dma((2, ZN, 3)),
             dma((2, ZN, 3)), dma((2, ZN, 3)),
             dma((2, ZN, 2)), dma((2, ZN, 2)),
             dma, dma,
             dma((64,)), dma,
-            dma((4,)), dma((4,)),
-            dma((4,)), dma((4,)),
-            dma((4,)), dma((4,)),
-            dma((6,)), dma((6,)),
+            dma((6, 4)), dma((6, 4)),
+            dma((2,)), dma((2,)),
             dma((7,)), dma((7,)),
             dma((7,)), dma((7,)),
             dma((13,)),
@@ -717,7 +748,7 @@
         ),
         name="axial_block",
     )(
-        tokens, cross_qkv, cross_out, depth_qkv, depth_out, gains, head_weight[None], head_bias[None],
+        tokens, cross_qkv.T, cross_out, depth_qkv.T, depth_out, gains, head_weight, head_bias,
         jnp.asarray(packing(), BF), enc, dep2, up_proj, down_proj,
     )
 

time: 150 us -> 130 us (0.87)
  Pallas kernels: 143 us -> 126 us
  local copies, waits for them, and re-layouts: 5.97 us -> 2.22 us
    pallas_call x1, Pallas kernels: 143 us -> 126 us  [body(): pl.pallas_call(block_kernel, out_shape=(jax.ShapeDtypeStruct((INL, XLD, D...]
    unnamed x8 -> x4, local copies, waits for them, and re-layouts: 4.71 us -> 2.22 us
where the time goes in v3:
time: 130 us
  Pallas kernels  126 us (97%)
  local copies, waits for them, and re-layouts  2.22 us (2%)
  between operations  1.3 us (1%)
    pallas_call x1, Pallas kernels, body(): pl.pallas_call(block_kernel, out_shape=(jax.ShapeDtypeStruct((INL, XLD, D...  126 us

profile of v3, /device:TPU:1, one launch (start us, length us, event | category | flops | bytes accessed | tf_op | source)
XLA Modules:
  0.0 129.8 jit_solution(3624772474473180329)
XLA Ops:
  1.3 126.3 %axial_block.1 = (bf16[4,4,8,768]{3,2,1,0:T(8,128)(2,1)}, f32[4,4,8]{2,1,0:T(4,128)}) custom-call(bf16[4,4,8,768]{3,2,1,0:T(8,128)(2,1)} %tok.1, bf16[36,768]{1,0:T(8,128)(2,1)} %bitcast.2, bf16[12,768]{1,0:T(8,128)(2,1)} %w2.1, bf16[36,768]{1,0:T(8,128)(2,1)} %bitcast.3, bf16[12,768]{1,0:T(8,128)(2,1)} %w4.1, f32[3,768]{1,0:T(4,128)} %gains.1, f32[768]{0:T(1024)} %head_w.1, ...), custom_call_target="tpu_custom_call" | custom-call | tf_op jit(solution)/shard_map/axial_block/pallas_call | solution.py:693
  127.6 0.0 copy-start
  127.6 1.6 %copy.18 = bf16[4,4,8,768]{3,2,1,0:T(8,128)(2,1)} copy(bf16[4,4,8,768]{3,2,1,0:T(8,128)(2,1)} %get-tuple-element.4) | data formatting | bytes 393216
  129.2 0.0 copy-done
  129.2 0.6 copy.19
Async XLA Ops:
  127.6 1.6 %copy-start = (f32[4,4,8]{2,1,0:T(4,128)S(1)}, f32[4,4,8]{2,1,0:T(4,128)}, u32[]{:S(2)}) copy-start(f32[4,4,8]{2,1,0:T(4,128)} %get-tuple-element.5) | copy-start | bytes 1540

commit v4 on v3

--- a/solution.py
+++ b/solution.py
@@ -22,6 +22,8 @@
 BLOCK = 2 * KIND
 QKV, SPAN = 3 * D, 4 * D
 PIECE, SUB = 48, 16
+LAG = 8
+STEPS = ZN - 1 + 3 * LAG
 SLOT = 48
 MESH = pl.DeviceIdType.MESH
 BF, F32 = jnp.bfloat16, jnp.float32
@@ -338,9 +340,9 @@
                 cp.start()
 
         stage(0, i, from_z)
-        stage(3, i, whole)
-        stage(6, i, lambda zsrc, _: collect_near(kind, zsrc))
-        stage(9, i, lambda zsrc, _: collect_far(kind, zsrc))
+        stage(LAG, i, whole)
+        stage(2 * LAG, i, lambda zsrc, _: collect_near(kind, zsrc))
+        stage(3 * LAG, i, lambda zsrc, _: collect_far(kind, zsrc))
 
     def siblings(kind):
         def one(zsrc, _):
@@ -428,14 +430,13 @@
             pltpu.make_async_copy(mine, mine, t_r).wait()
             l_copy().start()
 
-        @pl.when(i >= 18)
-        def _():
-            step(1, i - 18)
+        @pl.when(i >= STEPS - 15)
+        def _():
+            step(1, i - STEPS + 15)
 
         return 0
 
-    lax.fori_loop(0, 24, cross_step, 0)
-
+    lax.fori_loop(0, STEPS - 12, cross_step, 0)
     loads[0].wait()
     loads[1].wait()
     theirs = lines.at[rows16(32 * (1 - c), 32)]
@@ -449,6 +450,8 @@
     r = lax.broadcasted_iota(jnp.int32, (MINE, XL), 1)
     pick = jnp.where(r == 4 * (q // 2) + 2 * c + q % 2, 1.0, 0.0).astype(BF)
     nown[...] = jnp.dot(pick, nbuf[...], preferred_element_type=F32).astype(BF)
+
+    lax.fori_loop(STEPS - 12, STEPS, cross_step, 0)
 
     def attend(base, keys_in, queries_in, count, mask, between):
         def project(part, tokens_in, left):
@@ -486,7 +489,7 @@
         step(1, i)
         return 0
 
-    attend(0, nbuf, nown, XL, None, lambda p: depth_step(6 + p, 0))
+    attend(0, nbuf, nown, XL, None, lambda p: lax.fori_loop(15 + 2 * p, 17 + 2 * p, depth_step, 0))
     sendb[...] = obuf[...].T.reshape(GX, 2, D).astype(BF)
 
     def k_copy(i):
@@ -507,12 +510,18 @@
 
     lax.fori_loop(0, 64, k_start, 0)
 
-    lax.fori_loop(12, 24, depth_step, 0)
-    firsts(up_rings[1])
     seconds(down_ring)
     seconds(up_rings[0])
     firsts(down_spread[0])
     firsts(down_spread[1])
+    firsts(up_rings[1])
+    lax.fori_loop(27, STEPS, depth_step, 0)
+
+    finished(down_ring)
+    firsts(down_spread[2])
+    seconds(down_spread[0])
+    seconds(down_spread[1])
+    seconds(up_rings[1])
 
     own_c.wait()
     for d in range(1, 8):
@@ -540,12 +549,7 @@
         lax.broadcasted_iota(jnp.int32, (MINE, MINE), 0)
         + lax.broadcasted_iota(jnp.int32, (MINE, MINE), 1)
     ) % 2 == 0
-    finished(down_ring)
-    firsts(down_spread[2])
     siblings(1)
-    seconds(down_spread[0])
-    seconds(down_spread[1])
-    seconds(up_rings[1])
     attend(SPAN, nown, nown, MINE, mask, None)
     stream = stream + project_out(obuf[...].T.astype(BF), SPAN + QKV)
     nown[...] = normed(stream, gains[2:3, :])
@@ -604,6 +608,61 @@
     own_h.start()
     for d in range(1, 8):
         h_copy(d).start()
+    for d in range(1, 4):
+        y_copy(0, d).wait_send()
+        y_copy(1, d).wait_send()
+    for d in range(1, 8):
+        c_copy(d).wait_send()
+
+    def t_end(i, _):
+        @pl.when(jnp.logical_not(jnp.logical_and(32 * c + i == gx, own_line)))
+        def _():
+            t_copy(i).wait_send()
+
+        return 0
+
+    lax.fori_loop(0, 32, t_end, 0)
+
+    def k_end(i, _):
+        @pl.when(jnp.logical_not(jnp.logical_and(i == gx, me_too)))
+        def _():
+            k_copy(i).wait_send()
+
+        return 0
+
+    lax.fori_loop(0, 64, k_end, 0)
+    l_copy().wait_send()
+    for kind in range(2):
+        @pl.when(seat(z) < 3)
+        def _():
+            for d in range(1, ZN):
+                z_copy(kind, d).wait_send()
+
+        def w_end(k, _):
+            zsrc = (z + k) % ZN
+
+            @pl.when(k > 0)
+            def _():
+                @pl.when(seat(zsrc) < 3)
+                def _():
+                    for d in range(1, 4):
+                        x_copy(kind, zsrc, d).wait_send()
+
+                for cp in spread(kind, zsrc):
+                    cp.wait_send()
+                onward(kind, zsrc).wait_send()
+
+            for cp in relay(kind, zsrc):
+                cp.wait_send()
+            return 0
+
+        lax.fori_loop(0, ZN, w_end, 0)
+    for r in all_rings:
+        for n in range(2):
+            r[0](n).wait_send()
+            r[1](n).wait_send()
+    tok_copy().wait_send()
+    sum_copy().wait_send()
     own_f.wait()
     for d in range(1, 8):
         f_copy(d).wait_recv()
@@ -622,64 +681,9 @@
         picked = jnp.sum(jnp.where(mark, trecv[...], 0.0), 1)
         for n in range(GZ):
             time[n // 2, 2 * (n % 2) + k : 2 * (n % 2) + k + 1, :] = picked[n : n + 1, :DPD]
-
-    for d in range(1, 4):
-        y_copy(0, d).wait_send()
-        y_copy(1, d).wait_send()
-    for d in range(1, 8):
-        c_copy(d).wait_send()
+    for d in range(1, 8):
         f_copy(d).wait_send()
         h_copy(d).wait_send()
-
-    def t_end(i, _):
-        @pl.when(jnp.logical_not(jnp.logical_and(32 * c + i == gx, own_line)))
-        def _():
-            t_copy(i).wait_send()
-
-        return 0
-
-    lax.fori_loop(0, 32, t_end, 0)
-
-    def k_end(i, _):
-        @pl.when(jnp.logical_not(jnp.logical_and(i == gx, me_too)))
-        def _():
-            k_copy(i).wait_send()
-
-        return 0
-
-    lax.fori_loop(0, 64, k_end, 0)
-    l_copy().wait_send()
-    for kind in range(2):
-        @pl.when(seat(z) < 3)
-        def _():
-            for d in range(1, ZN):
-                z_copy(kind, d).wait_send()
-
-        def w_end(k, _):
-            zsrc = (z + k) % ZN
-
-            @pl.when(k > 0)
-            def _():
-                @pl.when(seat(zsrc) < 3)
-                def _():
-                    for d in range(1, 4):
-                        x_copy(kind, zsrc, d).wait_send()
-
-                for cp in spread(kind, zsrc):
-                    cp.wait_send()
-                onward(kind, zsrc).wait_send()
-
-            for cp in relay(kind, zsrc):
-                cp.wait_send()
-            return 0
-
-        lax.fori_loop(0, ZN, w_end, 0)
-    for r in all_rings:
-        for n in range(2):
-            r[0](n).wait_send()
-            r[1](n).wait_send()
-    tok_copy().wait_send()
-    sum_copy().wait_send()
 
 
 def body(

time: 130 us -> 114 us (0.88)
  Pallas kernels: 126 us -> 110 us
    pallas_call x1, Pallas kernels: 126 us -> 110 us  [body(): pl.pallas_call(block_kernel, out_shape=(jax.ShapeDtypeStruct((INL, XLD, D...]
where the time goes in v4:
time: 114 us
  Pallas kernels  110 us (96%)
  local copies, waits for them, and re-layouts  2.22 us (2%)
  between operations  1.3 us (1%)
    pallas_call x1, Pallas kernels, body(): pl.pallas_call(block_kernel, out_shape=(jax.ShapeDtypeStruct((INL, XLD, D...  110 us

profile of v4, /device:TPU:1, one launch (start us, length us, event | category | flops | bytes accessed | tf_op | source)
XLA Modules:
  0.0 113.8 jit_solution(676317143117314277)
XLA Ops:
  1.3 110.3 %axial_block.1 = (bf16[4,4,8,768]{3,2,1,0:T(8,128)(2,1)}, f32[4,4,8]{2,1,0:T(4,128)}) custom-call(bf16[4,4,8,768]{3,2,1,0:T(8,128)(2,1)} %tok.1, bf16[36,768]{1,0:T(8,128)(2,1)} %bitcast.2, bf16[12,768]{1,0:T(8,128)(2,1)} %w2.1, bf16[36,768]{1,0:T(8,128)(2,1)} %bitcast.3, bf16[12,768]{1,0:T(8,128)(2,1)} %w4.1, f32[3,768]{1,0:T(4,128)} %gains.1, f32[768]{0:T(1024)} %head_w.1, ...), custom_call_target="tpu_custom_call" | custom-call | tf_op jit(solution)/shard_map/axial_block/pallas_call | solution.py:697
  111.6 0.0 copy-start
  111.6 1.6 %copy.18 = bf16[4,4,8,768]{3,2,1,0:T(8,128)(2,1)} copy(bf16[4,4,8,768]{3,2,1,0:T(8,128)(2,1)} %get-tuple-element.4) | data formatting | bytes 393216
  113.2 0.0 copy-done
  113.2 0.6 copy.19
Async XLA Ops:
  111.6 1.6 %copy-start = (f32[4,4,8]{2,1,0:T(4,128)S(1)}, f32[4,4,8]{2,1,0:T(4,128)}, u32[]{:S(2)}) copy-start(f32[4,4,8]{2,1,0:T(4,128)} %get-tuple-element.5) | copy-start | bytes 1540

commit v5 on v4

--- a/solution.py
+++ b/solution.py
@@ -22,7 +22,7 @@
 BLOCK = 2 * KIND
 QKV, SPAN = 3 * D, 4 * D
 PIECE, SUB = 48, 16
-LAG = 8
+LAG = 6
 STEPS = ZN - 1 + 3 * LAG
 SLOT = 48
 MESH = pl.DeviceIdType.MESH
@@ -415,6 +415,7 @@
 
     firsts(down_ring)
     firsts(up_rings[0])
+    firsts(up_rings[1])
 
     def cross_step(i, _):
         step(0, i)
@@ -423,6 +424,12 @@
         def _():
             pack(1)
             begin(1)
+
+        @pl.when(i == 1)
+        def _():
+            seconds(down_ring)
+            firsts(down_spread[0])
+            firsts(down_spread[1])
 
         @pl.when(i == 10)
         def _():
@@ -510,18 +517,15 @@
 
     lax.fori_loop(0, 64, k_start, 0)
 
-    seconds(down_ring)
-    seconds(up_rings[0])
-    firsts(down_spread[0])
-    firsts(down_spread[1])
-    firsts(up_rings[1])
-    lax.fori_loop(27, STEPS, depth_step, 0)
-
     finished(down_ring)
     firsts(down_spread[2])
+    seconds(up_rings[0])
     seconds(down_spread[0])
     seconds(down_spread[1])
+    lax.fori_loop(27, STEPS, depth_step, 0)
+
     seconds(up_rings[1])
+    seconds(down_spread[2])
 
     own_c.wait()
     for d in range(1, 8):
@@ -560,7 +564,6 @@
     def sum_copy():
         return rcopy(sent, pair, a_s.at[1], a_r.at[1], gx, sib)
 
-    seconds(down_spread[2])
     tok_copy().start()
     pairtok[c] = nown[...]
     loads[2].wait()

time: 114 us -> 109 us (0.956)
  Pallas kernels: 110 us -> 105 us
    pallas_call x1, Pallas kernels: 110 us -> 105 us  [body(): pl.pallas_call(block_kernel, out_shape=(jax.ShapeDtypeStruct((INL, XLD, D...]
where the time goes in v5:
time: 109 us
  Pallas kernels  105 us (96%)
  local copies, waits for them, and re-layouts  2.22 us (2%)
  between operations  1.3 us (1%)
    pallas_call x1, Pallas kernels, body(): pl.pallas_call(block_kernel, out_shape=(jax.ShapeDtypeStruct((INL, XLD, D...  105 us
    unnamed x4, local copies, waits for them, and re-layouts  2.22 us

profile of v5, /device:TPU:1, one launch (start us, length us, event | category | flops | bytes accessed | tf_op | source)
XLA Modules:
  0.0 109.0 jit_solution(2766020684455230253)
XLA Ops:
  1.3 105.5 %axial_block.1 = (bf16[4,4,8,768]{3,2,1,0:T(8,128)(2,1)}, f32[4,4,8]{2,1,0:T(4,128)}) custom-call(bf16[4,4,8,768]{3,2,1,0:T(8,128)(2,1)} %tok.1, bf16[36,768]{1,0:T(8,128)(2,1)} %bitcast.2, bf16[12,768]{1,0:T(8,128)(2,1)} %w2.1, bf16[36,768]{1,0:T(8,128)(2,1)} %bitcast.3, bf16[12,768]{1,0:T(8,128)(2,1)} %w4.1, f32[3,768]{1,0:T(4,128)} %gains.1, f32[768]{0:T(1024)} %head_w.1, ...), custom_call_target="tpu_custom_call" | custom-call | tf_op jit(solution)/shard_map/axial_block/pallas_call | solution.py:700
  106.8 0.0 copy-start
  106.8 1.6 %copy.18 = bf16[4,4,8,768]{3,2,1,0:T(8,128)(2,1)} copy(bf16[4,4,8,768]{3,2,1,0:T(8,128)(2,1)} %get-tuple-element.4) | data formatting | bytes 393216
  108.4 0.0 copy-done
  108.4 0.6 copy.19
Async XLA Ops:
  106.8 1.6 %copy-start = (f32[4,4,8]{2,1,0:T(4,128)S(1)}, f32[4,4,8]{2,1,0:T(4,128)}, u32[]{:S(2)}) copy-start(f32[4,4,8]{2,1,0:T(4,128)} %get-tuple-element.5) | copy-start | bytes 1540
